TPU v7x, 128 devices: a whole 4x4x4 slice. The times are simulated.
128 devices in a mesh: samp: 8 (over z_hi, y), chrom: 16 (over x, z_lo, core).
Axes of the slice: x: 4, y: 4, z: 4 (z_hi: 2, z_lo: 2; z = z_hi * 2 + z_lo), core: 2. Of those that a mesh axis runs over, the one named last changes fastest.
Arguments:
- dosages: float32 [8192, 16384], P('samp', 'chrom'), may hold values from -12 to 12
- traits: float32 [8192, 128], P('samp'), may hold values from -14 to 14
- start_coef: float32 [16384, 128], P('chrom'), may hold values from -1 to 1
- groups: int32 [16384], P('chrom'), may hold values from 0 to 31, as said below
- tested: bfloat16 [8192, 16384], P('samp', 'chrom'), may hold values from -16 to 16
- owners: int32 [16384], P('chrom'), may hold values from 0 to 31, as said below
Outputs:
- scores: float32 [16384, 128], P('chrom')
- residual: float32 [8192, 128], P('samp')
Inputs may be any that keep to these rules, and one draw needn't show every extreme that they name: `groups`: training variant j belongs to group 2 * (j // 1024) + r with r from 0 to 1; every such group has a variant. `owners`: tested variant i belongs to group 2 * (i // 1024) + r with r from 0 to 1; every such group has a tested variant.
All inputs are finite; a program needn't handle non-finite values.
Results may differ from a plain program's by a relative error of at most 0.00045.
The roundings to bfloat16 on the way count: a program that leaves them out, or rounds other values in their place, can miss the bound.
Values sent between devices are 32-bit elements; how exact they have to be, the bound alone decides.
A program may use at most 64 MiB of HBM per device.

v0:
```python
import math

import jax
import jax.numpy as jnp
from jax import lax
from jax.sharding import PartitionSpec as P

GPD = 2
ITERS = 2


def matmul(left, right):
    return jnp.dot(left, right, precision=lax.Precision.HIGHEST, preferred_element_type=jnp.float32)


def inner_rows(left, right):
    return lax.dot_general(
        left,
        right,
        (((0,), (0,)), ((), ())),
        precision=lax.Precision.HIGHEST,
        preferred_element_type=jnp.float32,
    )


def total_prediction(partial_value):
    return lax.psum(partial_value, "chrom")


def body(dosages, traits, start_coef, groups, tested, owners):
    rows_dev = dosages.shape[0]
    total_rows = rows_dev * lax.axis_size("samp")
    penalty = 1.5 * math.sqrt(traits.shape[1] / total_rows)
    group_base = lax.axis_index("chrom") * GPD
    local_group = groups - group_base
    group_masks = [(local_group == which).astype(jnp.float32)[:, None] for which in range(GPD)]
    coefficients = start_coef
    for iteration in range(ITERS):
        prediction = total_prediction(matmul(dosages, coefficients))
        residual_now = traits - prediction
        gradient = lax.psum(inner_rows(dosages, residual_now) / total_rows, "samp")
        grad_sq = jnp.sum(gradient * gradient) / lax.axis_size("samp")
        image = lax.psum(matmul(dosages, gradient), "chrom")
        image_sq = jnp.sum(image * image) / lax.axis_size("chrom")
        grad_sq, image_sq = lax.psum((grad_sq, image_sq), ("samp", "chrom"))
        step_size = grad_sq / (image_sq / total_rows + 1e-06)
        moved_rows = coefficients + step_size * gradient
        length = jnp.sqrt(jnp.sum(moved_rows * moved_rows, axis=1, keepdims=True))
        coefficients = moved_rows * (
            jnp.maximum(length - step_size * penalty, 0.0)
            / jnp.maximum(length, step_size * penalty)
        )
    prediction = total_prediction(matmul(dosages, coefficients))
    own_parts = [matmul(dosages, coefficients * mask) for mask in group_masks]
    residual = traits - prediction
    tested_sq = jnp.sum(jnp.square(tested.astype(jnp.float32)), axis=0)
    picked = jnp.zeros((tested.shape[1], traits.shape[1]), jnp.float32)
    loco_list = []
    chosen_list = []
    for which in range(GPD):
        loco_resid = residual + own_parts[which]
        loco_list.append(jnp.sum(loco_resid * loco_resid, axis=0))
        products = lax.dot_general(
            tested,
            loco_resid.astype(jnp.bfloat16),
            (((0,), (0,)), ((), ())),
            preferred_element_type=jnp.float32,
        )
        chosen = (owners - group_base == which).astype(jnp.float32)[:, None]
        chosen_list.append(chosen)
        picked = picked + chosen * products
    picked, tested_sq, loco_all = lax.psum((picked, tested_sq, jnp.stack(loco_list)), "samp")
    loco_pick = jnp.zeros_like(picked)
    for which in range(GPD):
        loco_pick = loco_pick + chosen_list[which] * loco_all[which][None, :]
    denom = math.sqrt(total_rows) * jnp.sqrt(
        (tested_sq[:, None] / total_rows + 1e-06) * (loco_pick / total_rows + 1e-06)
    )
    return (picked / denom, residual)


def solution(mesh):
    placed = (
        P("samp", "chrom"),
        P("samp", None),
        P("chrom", None),
        P("chrom"),
        P("samp", "chrom"),
        P("chrom"),
    )
    return jax.shard_map(
        body,
        mesh=mesh,
        in_specs=placed,
        out_specs=(P("chrom", None), P("samp", None)),
        check_vma=False,
    )
```

profile of v0, /device:TPU:1, one launch (start us, length us, event | category | flops | bytes accessed | tf_op | source)
XLA Modules:
  0.0 1063.5 jit_solution(10045863915613818373)
XLA Ops:
  7.2 6.6 fusion.22
  13.9 121.9 %all-reduce.12.cloned.1.call-done = f32[1024,128]{1,0:T(8,128)} async-done(((f32[1024,128]{1,0:T(8,128)}), f32[1024,128]{1,0:T(8,128)}) %all-reduce.12.cloned.1.call-update) | async-done | bytes 524304 | tf_op jit(solution)/shard_map/psum | solution.py:27
  135.8 5.6 fusion
  141.4 81.2 %all-reduce.14.cloned.1.call-done = f32[1024,128]{0,1:T(8,128)} async-done(((f32[1024,128]{0,1:T(8,128)}), f32[1024,128]{0,1:T(8,128)}) %all-reduce.14.cloned.1.call-update) | async-done | bytes 524304 | tf_op jit(solution)/shard_map/psum | solution.py:41
  222.7 7.6 convolution_bitcast_fusion.5
  230.3 0.7 multiply_reduce_fusion.8
  231.7 121.0 %all-reduce.16.cloned.1.call-done = f32[1024,128]{0,1:T(8,128)} async-done(((f32[1024,128]{0,1:T(8,128)}), f32[1024,128]{0,1:T(8,128)}) %all-reduce.16.cloned.1.call-update) | async-done | bytes 524304 | tf_op jit(solution)/shard_map/psum | solution.py:43
  352.7 1.8 multiply_reduce_fusion.7
  355.3 67.3 %all-reduce.1 = (f32[]{:T(128)}, f32[]{:T(128)}) all-reduce(f32[]{:T(128)S(6)} %div.64, f32[]{:T(128)S(6)} %div.65), channel_id=1, replica_groups=mesh['samp'=8,'chrom'=16] {'samp','chrom'}, use_global_device_ids=true, to_apply=%region_3.0 | all-reduce | flops 2 | bytes 16 | tf_op jit(solution)/shard_map/psum | solution.py:45
  424.1 6.4 convolution_bitcast_fusion.4
  430.6 115.4 %all-reduce.18.cloned.1.call-done = f32[1024,128]{1,0:T(8,128)} async-done(((f32[1024,128]{1,0:T(8,128)}), f32[1024,128]{1,0:T(8,128)}) %all-reduce.18.cloned.1.call-update) | async-done | bytes 524304 | tf_op jit(solution)/shard_map/psum | solution.py:27
  545.9 5.6 fusion.1
  551.6 81.2 %all-reduce.20.cloned.1.call-done = f32[1024,128]{0,1:T(8,128)} async-done(((f32[1024,128]{0,1:T(8,128)}), f32[1024,128]{0,1:T(8,128)}) %all-reduce.20.cloned.1.call-update) | async-done | bytes 524304 | tf_op jit(solution)/shard_map/psum | solution.py:41
  632.8 7.6 convolution_bitcast_fusion.3
  640.5 0.7 multiply_reduce_fusion.5
  641.9 120.9 %all-reduce.22.cloned.1.call-done = f32[1024,128]{0,1:T(8,128)} async-done(((f32[1024,128]{0,1:T(8,128)}), f32[1024,128]{0,1:T(8,128)}) %all-reduce.22.cloned.1.call-update) | async-done | bytes 524304 | tf_op jit(solution)/shard_map/psum | solution.py:43
  762.8 1.8 multiply_reduce_fusion.4
  765.2 67.3 %all-reduce = (f32[]{:T(128)}, f32[]{:T(128)}) all-reduce(f32[]{:T(128)S(6)} %div.71, f32[]{:T(128)S(6)} %div.72), channel_id=1, replica_groups=mesh['samp'=8,'chrom'=16] {'samp','chrom'}, use_global_device_ids=true, to_apply=%region_11.0 | all-reduce | flops 2 | bytes 16 | tf_op jit(solution)/shard_map/psum | solution.py:45
  833.9 1.3 multiply_reduce_fusion.3
  835.2 7.3 convolution_bitcast_fusion.2
  842.7 2.0 copy.9
  844.7 0.5 multiply_reduce_fusion
  845.2 112.8 %all-reduce.24.cloned.1.call-done = f32[1024,128]{0,1:T(8,128)} async-done(((f32[1024,128]{0,1:T(8,128)}), f32[1024,128]{0,1:T(8,128)}) %all-reduce.24.cloned.1.call-update) | async-done | bytes 524304 | tf_op jit(solution)/shard_map/psum | solution.py:27
  958.0 1.3 sub.51
  959.2 1.0 copy.11
  960.2 6.7 multiply_reduce_fusion.1
  966.9 4.4 multiply_reduce_fusion.2
  971.8 1.3 fusion.3
  973.1 20.5 %all-reduce.2 = (f32[2,128]{1,0:T(2,128)S(1)}, f32[1024]{0:T(1024)S(1)}) all-reduce(f32[2,128]{1,0:T(2,128)S(1)} %pad_maximum_fusion, f32[1024]{0:T(1024)S(1)} %multiply_reduce_fusion), channel_id=1, replica_groups=mesh['samp'=8,'chrom'=16] {'samp'}, use_global_device_ids=true, to_apply=%region_22.0 | all-reduce | flops 1280 | bytes 10240 | tf_op jit(solution)/shard_map/psum | solution.py:72
  993.6 60.7 %all-reduce.26.cloned.1.call-done = f32[1024,128]{0,1:T(8,128)} async-done(((f32[1024,128]{0,1:T(8,128)}), f32[1024,128]{0,1:T(8,128)}) %all-reduce.26.cloned.1.call-update) | async-done | bytes 524304 | tf_op jit(solution)/shard_map/psum | solution.py:72
  1054.3 1.4 multiply_divide_fusion
  1055.7 1.0 copy.10
  (42 shorter events, 1.3 us)
Async XLA Ops:
  7.2 128.6 %copy-start.4 = (f32[1024,128]{1,0:T(8,128)S(1)}, f32[1024,128]{1,0:T(8,128)}, u32[]{:S(2)}) copy-start(f32[1024,128]{1,0:T(8,128)} %param.7) | copy-start | bytes 1572868
  7.2 128.6 %all-reduce.12.cloned.1.call-start = ((), (), s32[]{:S(2)}) async-start(), calls=%async_computation | async-start | bytes 1048576 | tf_op jit(solution)/shard_map/psum | solution.py:27
  13.8 208.9 %all-reduce.14.cloned.1.call-start = ((), (), s32[]{:S(2)}) async-start(), calls=%async_computation.1 | async-start | bytes 1048576 | tf_op jit(solution)/shard_map/psum | solution.py:41
  141.3 213.8 %copy-start.5 = (f32[1024,128]{1,0:T(8,128)S(1)}, f32[1024,128]{1,0:T(8,128)}, u32[]{:S(2)}) copy-start(f32[1024,128]{1,0:T(8,128)} %param.8) | copy-start | bytes 1572868
  141.4 211.3 %all-reduce.16.cloned.1.call-start = ((), (), s32[]{:S(2)}) async-start(), calls=%async_computation.2 | async-start | bytes 1048576 | tf_op jit(solution)/shard_map/psum | solution.py:43
  222.7 7.7 copy-start.3
  230.3 315.6 %all-reduce.18.cloned.1.call-start = ((), (), s32[]{:S(2)}) async-start(), calls=%async_computation.3 | async-start | bytes 1048576 | tf_op jit(solution)/shard_map/psum | solution.py:27
  430.5 202.3 %all-reduce.20.cloned.1.call-start = ((), (), s32[]{:S(2)}) async-start(), calls=%async_computation.4 | async-start | bytes 1048576 | tf_op jit(solution)/shard_map/psum | solution.py:41
  551.5 211.3 %all-reduce.22.cloned.1.call-start = ((), (), s32[]{:S(2)}) async-start(), calls=%async_computation.5 | async-start | bytes 1048576 | tf_op jit(solution)/shard_map/psum | solution.py:43
  632.8 7.7 copy-start.2
  640.4 317.6 %all-reduce.24.cloned.1.call-start = ((), (), s32[]{:S(2)}) async-start(), calls=%async_computation.6 | async-start | bytes 1048576 | tf_op jit(solution)/shard_map/psum | solution.py:27
  640.5 202.1 %copy-start.6 = (s32[1024]{0:T(1024)S(1)}, s32[1024]{0:T(1024)}, u32[]{:S(2)}) copy-start(s32[1024]{0:T(1024)} %param.9) | copy-start | bytes 12292
  833.9 10.8 %copy-start.7 = (s32[1024]{0:T(1024)S(1)}, s32[1024]{0:T(1024)}, u32[]{:S(2)}) copy-start(s32[1024]{0:T(1024)} %param.11) | copy-start | bytes 12292
  833.9 10.8 %copy-start.1 = (bf16[1024,1024]{1,0:T(8,128)(2,1)S(1)}, bf16[1024,1024]{1,0:T(8,128)(2,1)}, u32[]{:S(2)}) copy-start(bf16[1024,1024]{1,0:T(8,128)(2,1)} %param.10) | copy-start | bytes 6291460
  842.6 211.7 %all-reduce.26.cloned.1.call-start = ((), (), s32[]{:S(2)}) async-start(), calls=%async_computation.7 | async-start | bytes 1048576 | tf_op jit(solution)/shard_map/psum | solution.py:72
  960.2 6.7 copy-start
Sparse Core Ops, SparseCore 0:
  13.9 121.8 all-reduce.11
  141.5 81.1 all-reduce.13
  230.4 122.2 all-reduce.15
  430.6 115.2 all-reduce.17
  551.6 81.1 all-reduce.19
  640.5 122.2 all-reduce.21
  842.7 115.2 all-reduce.23
  973.2 81.0 all-reduce.25
where the time goes:
time: 1070 us; the launch traced here: 1060 us
  waiting for transfers between devices  815 us (76%)
  blocking collectives  155 us (14%)
  matrix products  59.3 us (6%)
  between operations  19.5 us (2%)
    psum x3, waiting for transfers between devices, total_prediction(): return lax.psum(partial_value, 'chrom')  350 us
    psum x2, waiting for transfers between devices, body(): image = lax.psum(matmul(dosages, gradient), 'chrom')  242 us
    psum x2, waiting for transfers between devices, body(): gradient = lax.psum(inner_rows(dosages, residual_now) / total_rows, 'samp')  162 us
    psum x2, blocking collectives, body(): grad_sq, image_sq = lax.psum((grad_sq, image_sq), ('samp', 'chrom'))  135 us
    psum x1, waiting for transfers between devices, body(): lax.psum((picked, tested_sq, jnp.stack(loco_list)), 'samp')  60.7 us
    dot_general x7, matrix products, matmul(): jnp.dot(left, right, precision=lax.Precision.HIGHEST, preferred_element_t...  46.5 us
  transfers between devices with their start and end apart: 8, of which 8 were waited for; matrix products, arithmetic and copies ran while one was open for 0% of the time, Pallas kernels for 0%

commit v1 on v0

v1 whole, which is shorter than its diff:
```python
import math

import jax
import jax.numpy as jnp
from jax import lax
from jax.experimental import pallas as pl
from jax.experimental.pallas import tpu as pltpu
from jax.sharding import PartitionSpec as P

MESH = pl.DeviceIdType.MESH
F32 = jnp.float32
BF16 = jnp.bfloat16
ITERS = 2
ROWS = 1024
K = 128
N = 8192
PENALTY = 1.5 * math.sqrt(K / N)


def remote(src, dst, send_sem, recv_sem, dev):
    return pltpu.make_async_remote_copy(
        src_ref=src, dst_ref=dst, send_sem=send_sem, recv_sem=recv_sem, device_id=dev, device_id_type=MESH
    )


def wait_bytes(ref, sem):
    pltpu.make_async_copy(ref, ref, sem).wait()


def split(value):
    high = value.astype(BF16)
    low = (value - high.astype(F32)).astype(BF16)
    return high, low


def kernel(
    dos_hbm, traits_hbm, coef_hbm, groups_ref, tested_hbm, owners_ref,
    scores_ref, resid_ref,
    dos, traits, coef, tested, ds, dts, tts, weights, loco_w,
    part, coresum, corebuf, crecv, rfull, gpart, grecv, gfull,
    own0, own1, gmask, omask, tsq, tsq_recv, lsq, lsq_recv, scal,
    load_sem, core_send, core_recv, crs_send, crs_recv, cag_send, cag_recv, fwd_send, fwd_recv,
    srs_send, srs_recv, sag_send, sag_recv, scal_send, scal_recv, small_send, small_recv,
):
    s = lax.axis_index("samp")
    c = lax.axis_index("chrom")
    core = c % 2
    other = 1 - core
    q = c // 2
    x = q // 2
    z = q % 2
    me = s * 16 + c
    partner = (s, q * 2 + other)

    order = [(other, 1 - x // 2), (other, x // 2), (core, 1 - x // 2), (core, x // 2)]
    load_coef = pltpu.make_async_copy(coef_hbm, coef, load_sem.at[0])
    load_coef.start()
    load_dos = []
    for i, (half, far) in enumerate(order):
        rows = pl.ds((half * 2 + far) * 256, 256)
        cp = pltpu.make_async_copy(dos_hbm.at[rows], dos.at[rows], load_sem.at[1 + i])
        cp.start()
        load_dos.append(cp)
    load_traits = pltpu.make_async_copy(traits_hbm, traits, load_sem.at[5])
    load_traits.start()
    load_tested = pltpu.make_async_copy(tested_hbm, tested, load_sem.at[6])
    load_tested.start()

    bar = pltpu.get_barrier_semaphore()

    @pl.loop(1, 128)
    def _(k):
        t = (me + k) % 128
        pl.semaphore_signal(bar, inc=1, device_id=(t // 16, t % 16), device_id_type=MESH)

    def set_weights(value, at=0):
        high, low = split(value)
        weights[:, at:at + K] = high
        weights[:, at + K:at + 2 * K] = low

    def chunk_dot(lhs, chunk, rhs):
        out = jnp.dot(lhs[chunk], rhs, preferred_element_type=F32)
        return (out[:256, :K] + (out[:256, K:] + out[256:, K:])) + out[256:, :K]

    def chrom_rs(ph, compute, filler=None):
        for i, (half, far) in enumerate(order):
            chunk = half * 2 + far
            value = compute(i, chunk)
            if i < 2:
                part[ph, i] = value
                remote(part.at[ph, i], corebuf.at[ph, i], core_send.at[ph, i], core_recv.at[ph, i], partner).start()
            else:
                part[ph, i] = value
        for i in range(2):
            far = order[i][1]
            wait_bytes(corebuf.at[ph, i], core_recv.at[ph, i])
            coresum[ph, pl.ds(far * 256, 256), :] = part[ph, 2 + i] + corebuf[ph, i]
            for j in range(4):
                t = far * 4 + j

                @pl.when(t != q)
                def _():
                    remote(
                        coresum.at[ph, pl.ds(t * 64, 64)], crecv.at[ph, q],
                        crs_send.at[ph], crs_recv.at[ph], (s, t * 2 + core),
                    ).start()
        crecv[ph, q] = coresum[ph, pl.ds(pl.multiple_of(q * 64, 64), 64), :]
        if filler is not None:
            filler()
        wait_bytes(crecv.at[ph, pl.ds(0, 7)], crs_recv.at[ph])
        total = crecv[ph, 0]
        for k in range(1, 8):
            total = total + crecv[ph, k]
        return total

    near = [(0, 1), (1, 0), (3, 0), (1, 1), (3, 1), (2, 0), (2, 1)]

    def chrom_ag(a, full, filler=None):
        base = core * 512
        mine = pl.ds(pl.multiple_of(base + q * 64, 64), 64)
        for dx, dz in reversed(near):
            t = (x + dx) % 4 * 2 + (z + dz) % 2
            remote(full.at[mine], full.at[mine], cag_send.at[a], cag_recv.at[a, q], (s, t * 2 + core)).start()
        remote(full.at[mine], full.at[mine], fwd_send.at[a], fwd_recv.at[a], partner).start()
        if filler is not None:
            filler()
        for dx, dz in near:
            t = (x + dx) % 4 * 2 + (z + dz) % 2
            rows = pl.ds(pl.multiple_of(base + t * 64, 64), 64)
            wait_bytes(full.at[rows], cag_recv.at[a, t])
            remote(full.at[rows], full.at[rows], fwd_send.at[a], fwd_recv.at[a], partner).start()
        wait_bytes(full.at[pl.ds(0, 512)], fwd_recv.at[a])

    def samp_rs(ph, compute, filler=None):
        for j in range(4):
            chunk = (s // 2 + 1 + j) % 4
            gpart[ph, pl.ds(pl.multiple_of(chunk * 256, 256), 256), :] = compute(chunk)
            for k in range(2):
                t = chunk * 2 + k

                @pl.when(t != s)
                def _():
                    remote(
                        gpart.at[ph, pl.ds(t * 128, 128)], grecv.at[ph, s],
                        srs_send.at[ph], srs_recv.at[ph], (t, c),
                    ).start()
        grecv[ph, s] = gpart[ph, pl.ds(pl.multiple_of(s * 128, 128), 128), :]
        if filler is not None:
            filler()
        wait_bytes(grecv.at[ph, pl.ds(0, 7)], srs_recv.at[ph])
        total = grecv[ph, 0]
        for k in range(1, 8):
            total = total + grecv[ph, k]
        return total

    def samp_ag(ph, full, filler=None):
        mine = pl.ds(pl.multiple_of(s * 128, 128), 128)
        for k in (6, 2, 5, 7, 3, 1, 4):
            t = (s // 4 + k // 4) % 2 * 4 + (s + k) % 4
            remote(full.at[mine], full.at[mine], sag_send.at[ph], sag_recv.at[ph], (t, c)).start()
        if filler is not None:
            filler()
        wait_bytes(full.at[pl.ds(0, 896)], sag_recv.at[ph])

    def prepare_transposed():
        @pl.loop(0, 16)
        def _(b):
            i, j = b // 4, b % 4
            rows = pl.ds(pl.multiple_of(i * 256, 256), 256)
            cols = pl.ds(pl.multiple_of(j * 256, 256), 256)
            high, low = split(dos[rows, cols].T)
            dts[j, 0:256, rows] = high
            dts[j, 256:512, rows] = low

    def prepare_tested():
        load_tested.wait()

        @pl.loop(0, 16)
        def _(b):
            i, j = b // 4, b % 4
            rows = pl.ds(pl.multiple_of(i * 256, 256), 256)
            cols = pl.ds(pl.multiple_of(j * 256, 256), 256)
            tts[j, :, rows] = tested[rows, cols].astype(F32).T.astype(BF16)

    def prepare_masks():
        for b in range(8):
            rows = slice(b * 128, b * 128 + 128)
            g = (groups_ref[b:b + 1, :] - c * 2).astype(F32)
            gmask[rows, :] = jnp.broadcast_to(g, (128, 128)).T
            o = (owners_ref[b:b + 1, :] - c * 2).astype(F32)
            omask[rows, :] = jnp.broadcast_to(o, (128, 128)).T

    def prepare_tsq():
        for b in range(8):
            def add(i, acc):
                value = tested[pl.ds(pl.multiple_of(i * 128, 128), 128), b * 128:(b + 1) * 128].astype(F32)
                return acc + jnp.sum((value * value).reshape(16, 8, 128), axis=0)
            acc = lax.fori_loop(0, 8, add, jnp.zeros((8, 128), F32))
            tsq[b:b + 1, :] = jnp.sum(acc, axis=0, keepdims=True)
        for k in range(1, 8):
            t = (s + k) % 8
            remote(tsq.at[pl.ds(t, 1)], tsq_recv.at[pl.ds(s, 1)], small_send.at[0], small_recv.at[0], (t, c)).start()
        tsq_recv[pl.ds(s, 1), :] = tsq[pl.ds(s, 1), :]

    load_coef.wait()
    set_weights(coef[...])

    def split_chunk(i, chunk):
        load_dos[i].wait()
        high, low = split(dos[pl.ds(pl.multiple_of(chunk * 256, 256), 256), :])
        ds[chunk, 0:256, :] = high
        ds[chunk, 256:512, :] = low

    def first_compute(i, chunk):
        split_chunk(i, chunk)
        if i == 0:
            pl.semaphore_wait(bar, 127)
        return chunk_dot(ds, chunk, weights[:, 0:256])

    def plain_compute(i, chunk):
        return chunk_dot(ds, chunk, weights[:, 0:256])

    lane = lax.broadcasted_iota(jnp.int32, (1, K), 1)
    shard64 = pl.ds(pl.multiple_of(core * 512 + q * 64, 64), 64)
    shard128 = pl.ds(pl.multiple_of(s * 128, 128), 128)

    for it in range(ITERS):
        total = chrom_rs(2 * it, first_compute if it == 0 else plain_compute,
                         prepare_transposed if it == 0 else None)
        if it == 0:
            load_traits.wait()
        rfull[it, shard64, :] = traits[shard64, :] - total
        chrom_ag(it, rfull.at[it])
        high, low = split(rfull[it])
        weights[:, 0:K] = high
        weights[:, K:2 * K] = low
        total = samp_rs(it, lambda chunk: chunk_dot(dts, chunk, weights[:, 0:256]),
                        prepare_masks if it == 1 else None)
        grad = total * (1.0 / N)
        gfull[it, shard128, :] = grad
        samp_ag(it, gfull.at[it], prepare_tested if it == 0 else prepare_tsq)
        set_weights(gfull[it])
        image = chrom_rs(2 * it + 1, plain_compute)
        g_row = jnp.sum(grad * grad, axis=0, keepdims=True)
        i_row = jnp.sum(image * image, axis=0, keepdims=True)
        g_row = g_row + pltpu.roll(g_row, 64, 1)
        i_row = i_row + pltpu.roll(i_row, 64, 1)
        scal[it, pl.ds(me, 1), :] = jnp.where(lane < 64, g_row, i_row)

        @pl.loop(1, 128)
        def _(k):
            t = (me + 128 - k) % 128
            remote(scal.at[it, pl.ds(me, 1)], scal.at[it, pl.ds(me, 1)], scal_send.at[it], scal_recv.at[it],
                   (t // 16, t % 16)).start()
        wait_bytes(scal.at[it, pl.ds(0, 127)], scal_recv.at[it])
        sums = jnp.sum(scal[it], axis=0, keepdims=True)
        grad_sq = jnp.sum(jnp.where(lane < 64, sums, 0.0), axis=1, keepdims=True)
        image_sq = jnp.sum(jnp.where(lane < 64, 0.0, sums), axis=1, keepdims=True)
        step = grad_sq / (image_sq * (1.0 / N) + 1e-06)
        moved = coef[...] + step * gfull[it]
        length = jnp.sqrt(jnp.sum(moved * moved, axis=1, keepdims=True))
        limit = step * PENALTY
        new = moved * (jnp.maximum(length - limit, 0.0) / jnp.maximum(length, limit))
        if it + 1 < ITERS:
            coef[...] = new
            set_weights(new)
        else:
            set_weights(new * (1.0 - gmask[...]), 0)
            set_weights(new * gmask[...], 256)

    def final_compute(i, chunk):
        rows = pl.ds(pl.multiple_of(chunk * 256, 256), 256)
        a = chunk_dot(ds, chunk, weights[:, 0:256])
        b = chunk_dot(ds, chunk, weights[:, 256:512])
        own0[rows, :] = a
        own1[rows, :] = b
        return a + b

    total = chrom_rs(4, final_compute)
    resid_ref[shard64, :] = traits[shard64, :] - total
    chrom_ag(2, resid_ref)
    res = resid_ref[...]
    loco0 = res + own0[...]
    loco1 = res + own1[...]
    lsq[0:1, :] = jnp.sum(loco0 * loco0, axis=0, keepdims=True)
    lsq[1:2, :] = jnp.sum(loco1 * loco1, axis=0, keepdims=True)
    loco_w[:, 0:K] = loco0.astype(BF16)
    loco_w[:, K:2 * K] = loco1.astype(BF16)
    for k in range(1, 8):
        t = (s + k) % 8
        remote(lsq, lsq_recv.at[s], small_send.at[1], small_recv.at[1], (t, c)).start()
    lsq_recv[s] = lsq[...]

    def products(chunk):
        out = jnp.dot(tts[chunk], loco_w[...], preferred_element_type=F32)
        which = omask[pl.ds(pl.multiple_of(chunk * 256, 256), 256), :]
        return jnp.where(which < 0.5, out[:, :K], out[:, K:])

    picked = samp_rs(2, products)
    wait_bytes(tsq_recv.at[pl.ds(0, 7)], small_recv.at[0])
    wait_bytes(lsq_recv.at[pl.ds(0, 7)], small_recv.at[1])
    tsum = jnp.sum(tsq_recv[...], axis=0, keepdims=True)
    tcol = jnp.broadcast_to(tsum, (128, 128)).T
    lsum = lsq_recv[0]
    for k in range(1, 8):
        lsum = lsum + lsq_recv[k]
    lpick = jnp.where(omask[shard128, :] < 0.5, lsum[0:1, :], lsum[1:2, :])
    denom = math.sqrt(N) * jnp.sqrt((tcol * (1.0 / N) + 1e-06) * (lpick * (1.0 / N) + 1e-06))
    scores_ref[shard128, :] = picked / denom
    samp_ag(2, scores_ref)

    for ph in range(5):
        for i in range(2):
            wait_bytes(corebuf.at[ph, i], core_send.at[ph, i])
        wait_bytes(crecv.at[ph, pl.ds(0, 7)], crs_send.at[ph])
    for a in range(3):
        wait_bytes(rfull.at[0, pl.ds(0, 448)], cag_send.at[a])
        wait_bytes(rfull.at[0, pl.ds(0, 512)], fwd_send.at[a])
        wait_bytes(grecv.at[a, pl.ds(0, 7)], srs_send.at[a])
        wait_bytes(gfull.at[0, pl.ds(0, 896)], sag_send.at[a])
    for it in range(ITERS):
        wait_bytes(scal.at[it, pl.ds(0, 127)], scal_send.at[it])
    wait_bytes(tsq_recv.at[pl.ds(0, 7)], small_send.at[0])
    wait_bytes(lsq_recv.at[pl.ds(0, 7)], small_send.at[1])


def body(dosages, traits, start_coef, groups, tested, owners):
    any_spec = pl.BlockSpec(memory_space=pl.ANY)
    vmem_spec = pl.BlockSpec(memory_space=pltpu.VMEM)
    V = pltpu.VMEM
    DMA = pltpu.SemaphoreType.DMA
    out = jax.ShapeDtypeStruct((ROWS, K), F32)
    return pl.pallas_call(
        kernel,
        out_shape=(out, out),
        in_specs=[any_spec, any_spec, any_spec, vmem_spec, any_spec, vmem_spec],
        out_specs=(vmem_spec, vmem_spec),
        scratch_shapes=[
            V((1024, 1024), F32), V((1024, K), F32), V((1024, K), F32), V((1024, 1024), BF16),
            V((4, 512, 1024), BF16), V((4, 512, 1024), BF16), V((4, 256, 1024), BF16),
            V((1024, 512), BF16), V((1024, 256), BF16),
            V((5, 4, 256, K), F32), V((5, 512, K), F32), V((5, 2, 256, K), F32), V((5, 8, 64, K), F32),
            V((2, 1024, K), F32), V((3, 1024, K), F32), V((3, 8, 128, K), F32), V((2, 1024, K), F32),
            V((1024, K), F32), V((1024, K), F32), V((1024, K), F32), V((1024, K), F32),
            V((8, K), F32), V((8, K), F32), V((2, K), F32), V((8, 2, K), F32), V((2, 128, K), F32),
            DMA((8,)), DMA((5, 2)), DMA((5, 2)), DMA((5,)), DMA((5,)), DMA((3,)), DMA((3, 8)), DMA((3,)), DMA((3,)),
            DMA((3,)), DMA((3,)), DMA((3,)), DMA((3,)), DMA((2,)), DMA((2,)), DMA((2,)), DMA((2,)),
        ],
        compiler_params=pltpu.CompilerParams(
            collective_id=0, has_side_effects=True, vmem_limit_bytes=60 * 1024 * 1024
        ),
    )(dosages, traits, start_coef, groups.reshape(8, 128), tested, owners.reshape(8, 128))


def solution(mesh):
    placed = (P("samp", "chrom"), P("samp", None), P("chrom", None), P("chrom"), P("samp", "chrom"), P("chrom"))
    return jax.shard_map(
        body, mesh=mesh, in_specs=placed, out_specs=(P("chrom", None), P("samp", None)), check_vma=False
    )
```

time: 1070 us -> 148 us (0.14)
  waiting for transfers between devices: 815 us -> 0 us
  blocking collectives: 155 us -> 0 us
  Pallas kernels: 0 us -> 143 us
  matrix products: 59.3 us -> 0 us
  between operations: 19.5 us -> 0.64 us
    psum x8 -> x0, waiting for transfers between devices: 815 us -> none  [the longest x3 350 us: total_prediction(): return lax.psum(partial_value, 'chrom')]
    psum x3 -> x0, blocking collectives: 155 us -> none  [the longest x2 135 us: body(): grad_sq, image_sq = lax.psum((grad_sq, image_sq), ('samp', 'chrom'))]
    pallas_call x0 -> x1, Pallas kernels: none -> 143 us  [body(): pl.pallas_call(kernel, out_shape=(out, out), in_specs=[any_spec, any_spec...]
    dot_general x11 -> x0, matrix products: 59.3 us -> none  [the longest x7 46.5 us: matmul(): jnp.dot(left, right, precision=lax.Precision.HIGHEST, preferred_element_t...]
  transfers between devices with their start and end apart: 8 -> 0, of which waited for: 8 -> 0; matrix products, arithmetic and copies ran while one was open for 0% -> 0% of each run, Pallas kernels for 0% -> 0%
where the time goes in v1:
time: 148 us; the launch traced here: 147 us
  Pallas kernels  143 us (97%)
  local copies, waits for them, and re-layouts  3.74 us (3%)
    pallas_call x1, Pallas kernels, body(): pl.pallas_call(kernel, out_shape=(out, out), in_specs=[any_spec, any_spec...  143 us
    unnamed x2, local copies, waits for them, and re-layouts  3.74 us

profile of v1, /device:TPU:1, one launch (start us, length us, event | category | flops | bytes accessed | tf_op | source)
XLA Modules:
  0.0 147.4 jit_solution(14269820965901100616)
XLA Ops:
  0.6 143.0 %shard_map.77 = (f32[1024,128]{1,0:T(8,128)}, f32[1024,128]{1,0:T(8,128)}) custom-call(f32[1024,1024]{1,0:T(8,128)} %dos_hbm.1, f32[1024,128]{1,0:T(8,128)} %traits_hbm.1, f32[1024,128]{1,0:T(8,128)} %coef_hbm.1, s32[8,128]{1,0:T(8,128)} %bitcast.2, bf16[1024,1024]{1,0:T(8,128)(2,1)} %tested_hbm.1, s32[8,128]{1,0:T(8,128)} %bitcast.3), custom_call_target="tpu_custom_call" | custom-call | tf_op jit(solution)/shard_map/pallas_call | solution.py:333
  143.6 1.9 %copy.10 = f32[1024,128]{1,0:T(8,128)} copy(f32[1024,128]{1,0:T(8,128)} %get-tuple-element.4) | data formatting | bytes 1048576
  145.5 1.9 %copy.11 = f32[1024,128]{1,0:T(8,128)} copy(f32[1024,128]{1,0:T(8,128)} %get-tuple-element.5) | data formatting | bytes 1048576

commit v2 on v1

v2 whole, which is shorter than its diff:
```python
import math

import jax
import jax.numpy as jnp
from jax import lax
from jax.experimental import pallas as pl
from jax.experimental.pallas import tpu as pltpu
from jax.sharding import PartitionSpec as P

MESH = pl.DeviceIdType.MESH
F32 = jnp.float32
BF16 = jnp.bfloat16
ITERS = 2
ROWS = 1024
K = 128
N = 8192
PENALTY = 1.5 * math.sqrt(K / N)


def remote(src, dst, send_sem, recv_sem, dev):
    return pltpu.make_async_remote_copy(
        src_ref=src, dst_ref=dst, send_sem=send_sem, recv_sem=recv_sem, device_id=dev, device_id_type=MESH
    )


def wait_bytes(ref, sem):
    pltpu.make_async_copy(ref, ref, sem).wait()


def split(value):
    high = value.astype(BF16)
    low = (value - high.astype(F32)).astype(BF16)
    return high, low


def kernel(
    dos_hbm, traits_hbm, coef_hbm, groups_ref, tested_hbm, owners_ref,
    scores_out, resid_out,
    dos, traits, coef, tested, ds, dts, tts, weights, loco_w,
    part, coresum, corebuf, crecv, rfull, gpart, grecv, gfull, score,
    own0, own1, gmask, omask, tcol, tsq_recv, lsq_recv, scal,
    load_sem, core_send, core_recv, far_send, crs_send, crs_recv, cag_send, cag_recv, fwd_send, fwd_recv,
    far_recv, srs_send, srs_recv, sag_send, sag_recv, scal_send, scal_recv, small_send, small_recv, out_sem,
):
    s = lax.axis_index("samp")
    c = lax.axis_index("chrom")
    core = c % 2
    other = 1 - core
    q = c // 2
    x = q // 2
    z = q % 2
    me = s * 16 + c
    partner = (s, q * 2 + other)
    opposite = (x + 2) % 4 * 2 + (1 - z)

    def chip(dx, dz):
        return (x + dx) % 4 * 2 + (z + dz) % 2

    def samp_peer(k):
        return (s // 4 + k // 4) % 2 * 4 + (s + k) % 4

    far_first = [(2, 0), (1, 1), (3, 1), (1, 0), (3, 0), (0, 1)]
    samp_order = (6, 2, 5, 7, 3, 1, 4)

    bar = pltpu.get_barrier_semaphore()
    for k in samp_order:
        pl.semaphore_signal(bar, inc=1, device_id=(samp_peer(k), c), device_id_type=MESH)
    for dx, dz in [(2, 1)] + far_first:
        pl.semaphore_signal(bar, inc=1, device_id=(s, chip(dx, dz) * 2 + core), device_id_type=MESH)
    pl.semaphore_signal(bar, inc=1, device_id=(s, opposite * 2 + other), device_id_type=MESH)
    pl.semaphore_signal(bar, inc=1, device_id=partner, device_id_type=MESH)

    order = [other * 2, other * 2 + 1, core * 2, core * 2 + 1]
    load_coef = pltpu.make_async_copy(coef_hbm, coef, load_sem.at[0])
    load_coef.start()
    load_dos = []
    for i, chunk in enumerate(order):
        rows = pl.ds(pl.multiple_of(chunk * 256, 256), 256)
        cp = pltpu.make_async_copy(dos_hbm.at[rows], dos.at[rows], load_sem.at[1 + i])
        cp.start()
        load_dos.append(cp)
    load_traits = pltpu.make_async_copy(traits_hbm, traits, load_sem.at[5])
    load_traits.start()
    load_tested = pltpu.make_async_copy(tested_hbm, tested, load_sem.at[6])
    load_tested.start()

    def set_weights(block, value, at=0):
        rows = slice(block * 128, block * 128 + 128)
        high, low = split(value)
        weights[rows, at:at + K] = high
        weights[rows, at + K:at + 2 * K] = low

    def blocks(ref):
        return [ref[b * 128:b * 128 + 128, :] for b in range(8)]

    def chunk_dot(lhs, chunk, rhs):
        out = jnp.dot(lhs[chunk], rhs, preferred_element_type=F32)
        return (out[:256, :K] + (out[:256, K:] + out[256:, K:])) + out[256:, :K]

    def rows32(t, u, half):
        return pl.ds(pl.multiple_of(half * 512 + u * 256 + t * 32, 32), 32)

    def chrom_rs(ph, compute, done, filler=None):
        cut = pl.ds(pl.multiple_of(opposite * 32, 32), 32)
        mine = pl.ds(pl.multiple_of(q * 32, 32), 32)
        for i, chunk in enumerate(order):
            u = i % 2
            part[ph, i] = compute(i, chunk)
            if i < 2:
                remote(part.at[ph, i], corebuf.at[ph, u], core_send.at[ph, u], core_recv.at[ph, u], partner).start()
                remote(part.at[ph, i, cut], crecv.at[ph, u, 8], far_send.at[ph], crs_recv.at[ph, u],
                       (s, opposite * 2 + other)).start()
            else:
                remote(part.at[ph, i, cut], crecv.at[ph, u, q], far_send.at[ph], crs_recv.at[ph, u],
                       (s, opposite * 2 + core)).start()
        for u in range(2):
            wait_bytes(corebuf.at[ph, u], core_recv.at[ph, u])
            coresum[ph, u] = part[ph, 2 + u] + corebuf[ph, u]
            for dx, dz in far_first:
                t = chip(dx, dz)
                remote(coresum.at[ph, u, pl.ds(pl.multiple_of(t * 32, 32), 32)], crecv.at[ph, u, q],
                       crs_send.at[ph], crs_recv.at[ph, u], (s, t * 2 + core)).start()
            crecv[ph, u, q] = coresum[ph, u, mine, :]
        if filler is not None:
            filler()
        for u in range(2):
            wait_bytes(crecv.at[ph, u, pl.ds(0, 8)], crs_recv.at[ph, u])
            total = crecv[ph, u, 0]
            for k in range(1, 9):
                total = total + crecv[ph, u, k]
            done(u, total)

    def chrom_ag_send(a, full, u):
        mine = rows32(q, u, core)
        remote(full.at[mine], full.at[mine], cag_send.at[a], cag_recv.at[a, u, q],
               (s, opposite * 2 + core)).start()
        remote(full.at[mine], full.at[mine], cag_send.at[a], far_recv.at[a, u],
               (s, opposite * 2 + other)).start()
        for dx, dz in far_first:
            remote(full.at[mine], full.at[mine], cag_send.at[a], cag_recv.at[a, u, q],
                   (s, chip(dx, dz) * 2 + core)).start()
        remote(full.at[mine], full.at[mine], fwd_send.at[a], fwd_recv.at[a, u], partner).start()

    def chrom_ag_wait(a, full):
        for u in range(2):
            for dx, dz in reversed(far_first):
                t = chip(dx, dz)
                rows = rows32(t, u, core)
                wait_bytes(full.at[rows], cag_recv.at[a, u, t])
                remote(full.at[rows], full.at[rows], fwd_send.at[a], fwd_recv.at[a, u], partner).start()
        for u in range(2):
            wait_bytes(full.at[rows32(0, u, core)], cag_recv.at[a, u, opposite])
            wait_bytes(full.at[rows32(0, u, core)], far_recv.at[a, u])
            wait_bytes(full.at[pl.ds(0, 224)], fwd_recv.at[a, u])

    def srows(t, u):
        return pl.ds(pl.multiple_of(u * 256 + t * 32, 32), 32)

    def samp_rs(ph, compute, done, filler=None):
        for u in range(4):
            gpart[ph, u] = compute(u)
            for k in samp_order:
                t = samp_peer(k)
                remote(gpart.at[ph, u, pl.ds(pl.multiple_of(t * 32, 32), 32)], grecv.at[ph, u, s],
                       srs_send.at[ph], srs_recv.at[ph, u], (t, c)).start()
            grecv[ph, u, s] = gpart[ph, u, pl.ds(pl.multiple_of(s * 32, 32), 32), :]
        if filler is not None:
            filler()
        for u in range(4):
            wait_bytes(grecv.at[ph, u, pl.ds(0, 7)], srs_recv.at[ph, u])
            total = grecv[ph, u, 0]
            for k in range(1, 8):
                total = total + grecv[ph, u, k]
            done(u, total)

    def samp_ag_send(ph, src, dst, u):
        for k in samp_order:
            remote(src, dst, sag_send.at[ph], sag_recv.at[ph, u], (samp_peer(k), c)).start()

    def samp_ag_wait(ph, u):
        wait_bytes(gfull.at[0, pl.ds(0, 224)], sag_recv.at[ph, u])

    def prepare_transposed():
        @pl.loop(0, 16)
        def _(b):
            i, j = b // 4, b % 4
            rows = pl.ds(pl.multiple_of(i * 256, 256), 256)
            cols = pl.ds(pl.multiple_of(j * 256, 256), 256)
            high, low = split(dos[rows, cols].T)
            dts[j, 0:256, rows] = high
            dts[j, 256:512, rows] = low

    def prepare_tested():
        @pl.loop(0, 16)
        def _(b):
            i, j = b // 4, b % 4
            rows = pl.ds(pl.multiple_of(i * 256, 256), 256)
            cols = pl.ds(pl.multiple_of(j * 256, 256), 256)
            tts[j, :, rows] = tested[rows, cols].astype(F32).T.astype(BF16)

    def prepare_tsq():
        load_tested.wait()
        for b in range(8):
            def add(i, acc):
                value = tested[pl.ds(pl.multiple_of(i * 128, 128), 128), b * 128:(b + 1) * 128].astype(F32)
                return acc + jnp.sum((value * value).reshape(16, 8, 128), axis=0)
            acc = lax.fori_loop(0, 8, add, jnp.zeros((8, 128), F32))
            tsq_recv[s, pl.ds(b, 1), :] = jnp.sum(acc, axis=0, keepdims=True)
        for k in samp_order:
            remote(tsq_recv.at[s], tsq_recv.at[s], small_send.at[0], small_recv.at[0], (samp_peer(k), c)).start()

    def prepare_masks():
        for b in range(8):
            rows = slice(b * 128, b * 128 + 128)
            g = (groups_ref[b:b + 1, :] - c * 2).astype(F32)
            gmask[rows, :] = jnp.broadcast_to(g, (128, 128)).T
            o = (owners_ref[b:b + 1, :] - c * 2).astype(F32)
            omask[rows, :] = jnp.broadcast_to(o, (128, 128)).T

    def prepare_tcol():
        wait_bytes(tsq_recv.at[pl.ds(0, 7)], small_recv.at[0])
        total = tsq_recv[0]
        for k in range(1, 8):
            total = total + tsq_recv[k]
        for b in range(8):
            tcol[b * 128:b * 128 + 128, :] = jnp.broadcast_to(total[b:b + 1, :], (128, 128)).T

    load_coef.wait()
    for b, value in enumerate(blocks(coef)):
        set_weights(b, value)

    def first_compute(i, chunk):
        load_dos[i].wait()
        high, low = split(dos[pl.ds(pl.multiple_of(chunk * 256, 256), 256), :])
        ds[chunk, 0:256, :] = high
        ds[chunk, 256:512, :] = low
        value = chunk_dot(ds, chunk, weights[:, 0:256])
        if i == 0:
            pl.semaphore_wait(bar, 16)
        return value

    def plain_compute(i, chunk):
        return chunk_dot(ds, chunk, weights[:, 0:256])

    lane = lax.broadcasted_iota(jnp.int32, (1, K), 1)

    for it in range(ITERS):
        def residual_done(u, total):
            if it == 0 and u == 0:
                load_traits.wait()
            rows = rows32(q, u, core)
            rfull[it, rows, :] = traits[rows, :] - total
            chrom_ag_send(it, rfull.at[it], u)

        chrom_rs(2 * it, first_compute if it == 0 else plain_compute, residual_done,
                 prepare_transposed if it == 0 else prepare_tcol)
        chrom_ag_wait(it, rfull.at[it])
        for b, value in enumerate(blocks(rfull.at[it])):
            set_weights(b, value)

        squares = []

        def gradient_done(u, total):
            grad = total * (1.0 / N)
            squares.append(jnp.sum(grad * grad, axis=0, keepdims=True))
            gfull[it, srows(s, u), :] = grad
            samp_ag_send(it, gfull.at[it, srows(s, u)], gfull.at[it, srows(s, u)], u)

        samp_rs(it, lambda u: chunk_dot(dts, u, weights[:, 0:256]), gradient_done,
                prepare_tsq if it == 0 else prepare_masks)
        if it == 0:
            prepare_tested()
        for u in range(4):
            samp_ag_wait(it, u)
            for b in (2 * u, 2 * u + 1):
                set_weights(b, gfull[it, b * 128:b * 128 + 128, :])
        g_row = (squares[0] + squares[1]) + (squares[2] + squares[3])
        g_row = g_row + pltpu.roll(g_row, 64, 1)
        image_squares = []
        chrom_rs(2 * it + 1, plain_compute,
                 lambda u, total: image_squares.append(jnp.sum(total * total, axis=0, keepdims=True)))
        i_row = image_squares[0] + image_squares[1]
        i_row = i_row + pltpu.roll(i_row, 64, 1)
        scal[it, pl.ds(me, 1), :] = jnp.where(lane < 64, g_row, i_row)

        @pl.loop(1, 128)
        def _(k):
            t = (me + 128 - k) % 128
            remote(scal.at[it, pl.ds(me, 1)], scal.at[it, pl.ds(me, 1)], scal_send.at[it], scal_recv.at[it],
                   (t // 16, t % 16)).start()
        wait_bytes(scal.at[it, pl.ds(0, 127)], scal_recv.at[it])
        sums = jnp.sum(scal[it], axis=0, keepdims=True)
        grad_sq = jnp.sum(jnp.where(lane < 64, sums, 0.0), axis=1, keepdims=True)
        image_sq = jnp.sum(jnp.where(lane < 64, 0.0, sums), axis=1, keepdims=True)
        step = grad_sq / (image_sq * (1.0 / N) + 1e-06)
        limit = step * PENALTY
        for b in range(8):
            rows = slice(b * 128, b * 128 + 128)
            moved = coef[rows, :] + step * gfull[it, rows, :]
            length = jnp.sqrt(jnp.sum(moved * moved, axis=1, keepdims=True))
            new = moved * (jnp.maximum(length - limit, 0.0) / jnp.maximum(length, limit))
            if it + 1 < ITERS:
                coef[rows, :] = new
                set_weights(b, new)
            else:
                second = new * gmask[rows, :]
                set_weights(b, new * (1.0 - gmask[rows, :]), 0)
                set_weights(b, second, 256)

    def final_compute(i, chunk):
        rows = pl.ds(pl.multiple_of(chunk * 256, 256), 256)
        a = chunk_dot(ds, chunk, weights[:, 0:256])
        b = chunk_dot(ds, chunk, weights[:, 256:512])
        own0[rows, :] = a
        own1[rows, :] = b
        return a + b

    def last_residual_done(u, total):
        rows = rows32(q, u, core)
        rfull[2, rows, :] = traits[rows, :] - total
        chrom_ag_send(2, rfull.at[2], u)

    chrom_rs(4, final_compute, last_residual_done)
    chrom_ag_wait(2, rfull.at[2])
    give_resid = pltpu.make_async_copy(rfull.at[2], resid_out, out_sem.at[0])
    give_resid.start()
    sq0 = jnp.zeros((1, K), F32)
    sq1 = jnp.zeros((1, K), F32)
    for b in range(8):
        rows = slice(b * 128, b * 128 + 128)
        res = rfull[2, rows, :]
        loco0 = res + own0[rows, :]
        loco1 = res + own1[rows, :]
        sq0 = sq0 + jnp.sum(loco0 * loco0, axis=0, keepdims=True)
        sq1 = sq1 + jnp.sum(loco1 * loco1, axis=0, keepdims=True)
        loco_w[rows, 0:K] = loco0.astype(BF16)
        loco_w[rows, K:2 * K] = loco1.astype(BF16)
    lsq_recv[s, 0:1, :] = sq0
    lsq_recv[s, 1:2, :] = sq1
    for k in samp_order:
        remote(lsq_recv.at[s], lsq_recv.at[s], small_send.at[1], small_recv.at[1], (samp_peer(k), c)).start()

    def products(u):
        out = jnp.dot(tts[u], loco_w[...], preferred_element_type=F32)
        return jnp.where(omask[u * 256:u * 256 + 256, :] < 0.5, out[:, :K], out[:, K:])

    def score_done(u, picked):
        if u == 0:
            wait_bytes(lsq_recv.at[pl.ds(0, 7)], small_recv.at[1])
        lsum = lsq_recv[0]
        for k in range(1, 8):
            lsum = lsum + lsq_recv[k]
        rows = srows(s, u)
        lpick = jnp.where(omask[rows, :] < 0.5, lsum[0:1, :], lsum[1:2, :])
        denom = math.sqrt(N) * jnp.sqrt((tcol[rows, :] * (1.0 / N) + 1e-06) * (lpick * (1.0 / N) + 1e-06))
        score[u] = picked / denom
        samp_ag_send(2, score.at[u], scores_out.at[rows], u)
        pltpu.make_async_copy(score.at[u], scores_out.at[rows], out_sem.at[1 + u]).start()

    samp_rs(2, products, score_done)
    for u in range(4):
        samp_ag_wait(2, u)
        wait_bytes(score.at[u], out_sem.at[1 + u])
    give_resid.wait()

    for ph in range(5):
        for u in range(2):
            wait_bytes(corebuf.at[ph, u], core_send.at[ph, u])
        wait_bytes(rfull.at[0, pl.ds(0, 128)], far_send.at[ph])
        wait_bytes(rfull.at[0, pl.ds(0, 384)], crs_send.at[ph])
    for a in range(3):
        wait_bytes(rfull.at[0, pl.ds(0, 512)], cag_send.at[a])
        wait_bytes(rfull.at[0, pl.ds(0, 448)], fwd_send.at[a])
        wait_bytes(rfull.at[0, pl.ds(0, 896)], srs_send.at[a])
        wait_bytes(rfull.at[0, pl.ds(0, 896)], sag_send.at[a])
    for it in range(ITERS):
        wait_bytes(scal.at[it, pl.ds(0, 127)], scal_send.at[it])
    wait_bytes(tsq_recv.at[pl.ds(0, 7)], small_send.at[0])
    wait_bytes(lsq_recv.at[pl.ds(0, 7)], small_send.at[1])


def hand_over_kernel(a_in, b_in, a_out, b_out, buf, in_sem, out_sem):
    pairs = [(a_in, a_out, i) for i in range(2)] + [(b_in, b_out, i) for i in range(2)]
    loads, stores = [], []
    for n, (src, _, i) in enumerate(pairs):
        loads.append(pltpu.make_async_copy(src.at[pl.ds(i * 512, 512)], buf.at[n], in_sem.at[n]))
        loads[-1].start()
    for n, (_, dst, i) in enumerate(pairs):
        loads[n].wait()
        stores.append(pltpu.make_async_copy(buf.at[n], dst.at[pl.ds(i * 512, 512)], out_sem.at[n]))
        stores[-1].start()
    for cp in stores:
        cp.wait()


def body(dosages, traits, start_coef, groups, tested, owners):
    any_spec = pl.BlockSpec(memory_space=pl.ANY)
    vmem_spec = pl.BlockSpec(memory_space=pltpu.VMEM)
    V = pltpu.VMEM
    DMA = pltpu.SemaphoreType.DMA
    out = jax.ShapeDtypeStruct((ROWS, K), F32)
    scores, resid = pl.pallas_call(
        kernel,
        out_shape=(out, out),
        in_specs=[any_spec, any_spec, any_spec, vmem_spec, any_spec, vmem_spec],
        out_specs=(any_spec, any_spec),
        scratch_shapes=[
            V((1024, 1024), F32), V((1024, K), F32), V((1024, K), F32), V((1024, 1024), BF16),
            V((4, 512, 1024), BF16), V((4, 512, 1024), BF16), V((4, 256, 1024), BF16),
            V((1024, 512), BF16), V((1024, 256), BF16),
            V((5, 4, 256, K), F32), V((5, 2, 256, K), F32), V((5, 2, 256, K), F32), V((5, 2, 9, 32, K), F32),
            V((3, 1024, K), F32), V((3, 4, 256, K), F32), V((3, 4, 8, 32, K), F32), V((2, 1024, K), F32),
            V((4, 32, K), F32),
            V((1024, K), F32), V((1024, K), F32), V((1024, K), F32), V((1024, K), F32), V((1024, K), F32),
            V((8, 8, K), F32), V((8, 2, K), F32), V((2, 128, K), F32),
            DMA((8,)), DMA((5, 2)), DMA((5, 2)), DMA((5,)), DMA((5,)), DMA((5, 2)), DMA((3,)), DMA((3, 2, 8)),
            DMA((3,)), DMA((3, 2)), DMA((3, 2)), DMA((3,)), DMA((3, 4)), DMA((3,)), DMA((3, 4)),
            DMA((2,)), DMA((2,)), DMA((2,)), DMA((2,)), DMA((5,)),
        ],
        compiler_params=pltpu.CompilerParams(
            collective_id=0, has_side_effects=True, vmem_limit_bytes=62 * 1024 * 1024
        ),
    )(dosages, traits, start_coef, groups.reshape(8, 128), tested, owners.reshape(8, 128))
    return pl.pallas_call(
        hand_over_kernel,
        out_shape=(out, out),
        in_specs=[any_spec, any_spec],
        out_specs=(any_spec, any_spec),
        scratch_shapes=[V((4, 512, K), F32), DMA((4,)), DMA((4,))],
    )(scores, resid)


def solution(mesh):
    placed = (P("samp", "chrom"), P("samp", None), P("chrom", None), P("chrom"), P("samp", "chrom"), P("chrom"))
    return jax.shard_map(
        body, mesh=mesh, in_specs=placed, out_specs=(P("chrom", None), P("samp", None)), check_vma=False
    )
```

time: 148 us -> 133 us (0.90)
  Pallas kernels: 143 us -> 132 us
  local copies, waits for them, and re-layouts: 3.74 us -> 0 us
    pallas_call x1, Pallas kernels: 143 us -> 130 us  [body(): pl.pallas_call(kernel, out_shape=(out, out), in_specs=[any_spec, any_spec...]
    unnamed x2 -> x0, local copies, waits for them, and re-layouts: 3.74 us -> none
    pallas_call x0 -> x1, Pallas kernels: none -> 1.98 us  [body(): pl.pallas_call(hand_over_kernel, out_shape=(out, out), in_specs=[any_spec...]
where the time goes in v2:
time: 133 us
  Pallas kernels  132 us (99%)
    pallas_call x1, Pallas kernels, body(): pl.pallas_call(kernel, out_shape=(out, out), in_specs=[any_spec, any_spec...  130 us

profile of v2, /device:TPU:1, one launch (start us, length us, event | category | flops | bytes accessed | tf_op | source)
XLA Modules:
  0.0 132.6 jit_solution(12671032831226135076)
XLA Ops:
  0.6 129.8 %shard_map.77 = (f32[1024,128]{1,0:T(8,128)}, f32[1024,128]{1,0:T(8,128)}) custom-call(f32[1024,1024]{1,0:T(8,128)} %dos_hbm.1, f32[1024,128]{1,0:T(8,128)} %traits_hbm.1, f32[1024,128]{1,0:T(8,128)} %coef_hbm.1, s32[8,128]{1,0:T(8,128)} %bitcast.2, bf16[1024,1024]{1,0:T(8,128)(2,1)} %tested_hbm.1, s32[8,128]{1,0:T(8,128)} %bitcast.3), custom_call_target="tpu_custom_call" | custom-call | tf_op jit(solution)/shard_map/pallas_call | solution.py:402
  130.5 2.0 %shard_map.78 = (f32[1024,128]{1,0:T(8,128)}, f32[1024,128]{1,0:T(8,128)}) custom-call(f32[1024,128]{1,0:T(8,128)} %get-tuple-element.4.a_in, f32[1024,128]{1,0:T(8,128)} %get-tuple-element.5.b_in), custom_call_target="tpu_custom_call" | custom-call | tf_op jit(solution)/shard_map/pallas_call | solution.py:424

commit v3 on v2

--- a/solution.py
+++ b/solution.py
@@ -38,7 +38,7 @@
     scores_out, resid_out,
     dos, traits, coef, tested, ds, dts, tts, weights, loco_w,
     part, coresum, corebuf, crecv, rfull, gpart, grecv, gfull, score,
-    own0, own1, gmask, omask, tcol, tsq_recv, lsq_recv, scal,
+    acc, own0, own1, gmask, omask, tcol, tsq_recv, lsq_recv, scal,
     load_sem, core_send, core_recv, far_send, crs_send, crs_recv, cag_send, cag_recv, fwd_send, fwd_recv,
     far_recv, srs_send, srs_recv, sag_send, sag_recv, scal_send, scal_recv, small_send, small_recv, out_sem,
 ):
@@ -62,6 +62,22 @@
     far_first = [(2, 0), (1, 1), (3, 1), (1, 0), (3, 0), (0, 1)]
     samp_order = (6, 2, 5, 7, 3, 1, 4)
 
+    y = s % 4
+    depth = s // 4 * 2 + z
+    steps = []
+    for dx in range(4):
+        for dy in range(4):
+            for dz in range(4):
+                for dc in range(2):
+                    if dx + dy + dz + dc:
+                        steps.append((-sum(min(d, 4 - d) for d in (dx, dy, dz)), dx, dy, dz, dc))
+    everyone = []
+    xs, ys, zs, cs = [[(v + d) % 4 for d in range(4)] for v in (x, y, depth)] + [[core, other]]
+    s_of = [[zz // 2 * 4 + yy for yy in ys] for zz in zs]
+    c_of = [[[xx * 4 + zz % 2 * 2 + cc for cc in cs] for xx in xs] for zz in zs]
+    for _, dx, dy, dz, dc in sorted(steps):
+        everyone.append((s_of[dz][dy], c_of[dz][dx][dc]))
+
     bar = pltpu.get_barrier_semaphore()
     for k in samp_order:
         pl.semaphore_signal(bar, inc=1, device_id=(samp_peer(k), c), device_id_type=MESH)
@@ -95,6 +111,13 @@
 
     def chunk_dot(lhs, chunk, rhs):
         out = jnp.dot(lhs[chunk], rhs, preferred_element_type=F32)
+        return (out[:256, :K] + (out[:256, K:] + out[256:, K:])) + out[256:, :K]
+
+    def rows256(chunk):
+        return pl.ds(pl.multiple_of(chunk * 256, 256), 256)
+
+    def part_dot(lhs, chunk, depth):
+        out = jnp.dot(lhs[chunk, :, depth], weights[depth, 0:256], preferred_element_type=F32)
         return (out[:256, :K] + (out[:256, K:] + out[256:, K:])) + out[256:, :K]
 
     def rows32(t, u, half):
@@ -141,17 +164,20 @@
                    (s, chip(dx, dz) * 2 + core)).start()
         remote(full.at[mine], full.at[mine], fwd_send.at[a], fwd_recv.at[a, u], partner).start()
 
-    def chrom_ag_wait(a, full):
+    def chrom_ag_wait(a, full, use):
         for u in range(2):
             for dx, dz in reversed(far_first):
                 t = chip(dx, dz)
                 rows = rows32(t, u, core)
                 wait_bytes(full.at[rows], cag_recv.at[a, u, t])
                 remote(full.at[rows], full.at[rows], fwd_send.at[a], fwd_recv.at[a, u], partner).start()
+            wait_bytes(full.at[rows32(0, u, core)], cag_recv.at[a, u, opposite])
+        use(core * 2)
+        use(core * 2 + 1)
         for u in range(2):
-            wait_bytes(full.at[rows32(0, u, core)], cag_recv.at[a, u, opposite])
             wait_bytes(full.at[rows32(0, u, core)], far_recv.at[a, u])
             wait_bytes(full.at[pl.ds(0, 224)], fwd_recv.at[a, u])
+            use(other * 2 + u)
 
     def srows(t, u):
         return pl.ds(pl.multiple_of(u * 256 + t * 32, 32), 32)
@@ -191,6 +217,8 @@
             dts[j, 256:512, rows] = low
 
     def prepare_tested():
+        load_tested.wait()
+
         @pl.loop(0, 16)
         def _(b):
             i, j = b // 4, b % 4
@@ -199,7 +227,6 @@
             tts[j, :, rows] = tested[rows, cols].astype(F32).T.astype(BF16)
 
     def prepare_tsq():
-        load_tested.wait()
         for b in range(8):
             def add(i, acc):
                 value = tested[pl.ds(pl.multiple_of(i * 128, 128), 128), b * 128:(b + 1) * 128].astype(F32)
@@ -253,10 +280,21 @@
             chrom_ag_send(it, rfull.at[it], u)
 
         chrom_rs(2 * it, first_compute if it == 0 else plain_compute, residual_done,
-                 prepare_transposed if it == 0 else prepare_tcol)
-        chrom_ag_wait(it, rfull.at[it])
-        for b, value in enumerate(blocks(rfull.at[it])):
-            set_weights(b, value)
+                 prepare_transposed if it == 0 else prepare_tsq)
+        seen = []
+
+        def use_residual(chunk):
+            rows = rows256(chunk)
+            high, low = split(rfull[it, rows, :])
+            weights[rows, 0:K] = high
+            weights[rows, K:2 * K] = low
+            seen.append(rows)
+            if len(seen) < 4:
+                for v in range(4):
+                    value = part_dot(dts, v, rows)
+                    acc[v, :, 0:K] = value if len(seen) == 1 else acc[v, :, 0:K] + value
+
+        chrom_ag_wait(it, rfull.at[it], use_residual)
 
         squares = []
 
@@ -266,28 +304,30 @@
             gfull[it, srows(s, u), :] = grad
             samp_ag_send(it, gfull.at[it, srows(s, u)], gfull.at[it, srows(s, u)], u)
 
-        samp_rs(it, lambda u: chunk_dot(dts, u, weights[:, 0:256]), gradient_done,
-                prepare_tsq if it == 0 else prepare_masks)
+        samp_rs(it, lambda v: acc[v, :, 0:K] + part_dot(dts, v, seen[3]), gradient_done,
+                prepare_masks if it == 0 else prepare_tcol)
         if it == 0:
             prepare_tested()
         for u in range(4):
             samp_ag_wait(it, u)
             for b in (2 * u, 2 * u + 1):
                 set_weights(b, gfull[it, b * 128:b * 128 + 128, :])
+            if u < 3:
+                for v in range(4):
+                    value = part_dot(ds, v, slice(u * 256, u * 256 + 256))
+                    acc[v, :, 0:K] = value if u == 0 else acc[v, :, 0:K] + value
         g_row = (squares[0] + squares[1]) + (squares[2] + squares[3])
         g_row = g_row + pltpu.roll(g_row, 64, 1)
         image_squares = []
-        chrom_rs(2 * it + 1, plain_compute,
+        chrom_rs(2 * it + 1, lambda i, chunk: acc[chunk, :, 0:K] + part_dot(ds, chunk, slice(768, 1024)),
                  lambda u, total: image_squares.append(jnp.sum(total * total, axis=0, keepdims=True)))
         i_row = image_squares[0] + image_squares[1]
         i_row = i_row + pltpu.roll(i_row, 64, 1)
         scal[it, pl.ds(me, 1), :] = jnp.where(lane < 64, g_row, i_row)
 
-        @pl.loop(1, 128)
-        def _(k):
-            t = (me + 128 - k) % 128
+        for far_s, far_c in everyone:
             remote(scal.at[it, pl.ds(me, 1)], scal.at[it, pl.ds(me, 1)], scal_send.at[it], scal_recv.at[it],
-                   (t // 16, t % 16)).start()
+                   (far_s, far_c)).start()
         wait_bytes(scal.at[it, pl.ds(0, 127)], scal_recv.at[it])
         sums = jnp.sum(scal[it], axis=0, keepdims=True)
         grad_sq = jnp.sum(jnp.where(lane < 64, sums, 0.0), axis=1, keepdims=True)
@@ -321,28 +361,39 @@
         chrom_ag_send(2, rfull.at[2], u)
 
     chrom_rs(4, final_compute, last_residual_done)
-    chrom_ag_wait(2, rfull.at[2])
-    give_resid = pltpu.make_async_copy(rfull.at[2], resid_out, out_sem.at[0])
-    give_resid.start()
-    sq0 = jnp.zeros((1, K), F32)
-    sq1 = jnp.zeros((1, K), F32)
-    for b in range(8):
-        rows = slice(b * 128, b * 128 + 128)
+    sq = []
+    seen_last = []
+
+    def use_last(chunk):
+        rows = rows256(chunk)
         res = rfull[2, rows, :]
         loco0 = res + own0[rows, :]
         loco1 = res + own1[rows, :]
-        sq0 = sq0 + jnp.sum(loco0 * loco0, axis=0, keepdims=True)
-        sq1 = sq1 + jnp.sum(loco1 * loco1, axis=0, keepdims=True)
+        sq.append((jnp.sum(loco0 * loco0, axis=0, keepdims=True), jnp.sum(loco1 * loco1, axis=0, keepdims=True)))
         loco_w[rows, 0:K] = loco0.astype(BF16)
         loco_w[rows, K:2 * K] = loco1.astype(BF16)
-    lsq_recv[s, 0:1, :] = sq0
-    lsq_recv[s, 1:2, :] = sq1
-    for k in samp_order:
-        remote(lsq_recv.at[s], lsq_recv.at[s], small_send.at[1], small_recv.at[1], (samp_peer(k), c)).start()
-
-    def products(u):
-        out = jnp.dot(tts[u], loco_w[...], preferred_element_type=F32)
-        return jnp.where(omask[u * 256:u * 256 + 256, :] < 0.5, out[:, :K], out[:, K:])
+        seen_last.append(rows)
+        if len(seen_last) < 4:
+            for v in range(4):
+                value = products_of(v, rows)
+                acc[v] = value if len(seen_last) == 1 else acc[v] + value
+
+    def products_of(v, depth):
+        return jnp.dot(tts[v, :, depth], loco_w[depth, :], preferred_element_type=F32)
+
+    chrom_ag_wait(2, rfull.at[2], use_last)
+    give_resid = pltpu.make_async_copy(rfull.at[2], resid_out, out_sem.at[0])
+    give_resid.start()
+
+    def products(v):
+        out = acc[v] + products_of(v, seen_last[3])
+        return jnp.where(omask[v * 256:v * 256 + 256, :] < 0.5, out[:, :K], out[:, K:])
+
+    def send_squares():
+        lsq_recv[s, 0:1, :] = (sq[0][0] + sq[1][0]) + (sq[2][0] + sq[3][0])
+        lsq_recv[s, 1:2, :] = (sq[0][1] + sq[1][1]) + (sq[2][1] + sq[3][1])
+        for k in samp_order:
+            remote(lsq_recv.at[s], lsq_recv.at[s], small_send.at[1], small_recv.at[1], (samp_peer(k), c)).start()
 
     def score_done(u, picked):
         if u == 0:
@@ -357,7 +408,7 @@
         samp_ag_send(2, score.at[u], scores_out.at[rows], u)
         pltpu.make_async_copy(score.at[u], scores_out.at[rows], out_sem.at[1 + u]).start()
 
-    samp_rs(2, products, score_done)
+    samp_rs(2, products, score_done, send_squares)
     for u in range(4):
         samp_ag_wait(2, u)
         wait_bytes(score.at[u], out_sem.at[1 + u])
@@ -410,7 +461,7 @@
             V((1024, 512), BF16), V((1024, 256), BF16),
             V((5, 4, 256, K), F32), V((5, 2, 256, K), F32), V((5, 2, 256, K), F32), V((5, 2, 9, 32, K), F32),
             V((3, 1024, K), F32), V((3, 4, 256, K), F32), V((3, 4, 8, 32, K), F32), V((2, 1024, K), F32),
-            V((4, 32, K), F32),
+            V((4, 32, K), F32), V((4, 256, 2 * K), F32),
             V((1024, K), F32), V((1024, K), F32), V((1024, K), F32), V((1024, K), F32), V((1024, K), F32),
             V((8, 8, K), F32), V((8, 2, K), F32), V((2, 128, K), F32),
             DMA((8,)), DMA((5, 2)), DMA((5, 2)), DMA((5,)), DMA((5,)), DMA((5, 2)), DMA((3,)), DMA((3, 2, 8)),

time: 133 us -> 129 us (0.970)
  Pallas kernels: 132 us -> 128 us
    pallas_call x1, Pallas kernels: 130 us -> 126 us  [body(): pl.pallas_call(kernel, out_shape=(out, out), in_specs=[any_spec, any_spec...]
where the time goes in v3:
time: 129 us
  Pallas kernels  128 us (99%)
    pallas_call x1, Pallas kernels, body(): pl.pallas_call(kernel, out_shape=(out, out), in_specs=[any_spec, any_spec...  126 us

profile of v3, /device:TPU:1, one launch (start us, length us, event | category | flops | bytes accessed | tf_op | source)
XLA Modules:
  0.0 129.1 jit_solution(1845902456422355523)
XLA Ops:
  0.6 126.3 %shard_map.77 = (f32[1024,128]{1,0:T(8,128)}, f32[1024,128]{1,0:T(8,128)}) custom-call(f32[1024,1024]{1,0:T(8,128)} %dos_hbm.1, f32[1024,128]{1,0:T(8,128)} %traits_hbm.1, f32[1024,128]{1,0:T(8,128)} %coef_hbm.1, s32[8,128]{1,0:T(8,128)} %bitcast.2, bf16[1024,1024]{1,0:T(8,128)(2,1)} %tested_hbm.1, s32[8,128]{1,0:T(8,128)} %bitcast.3), custom_call_target="tpu_custom_call" | custom-call | tf_op jit(solution)/shard_map/pallas_call | solution.py:453
  126.9 2.0 %shard_map.78 = (f32[1024,128]{1,0:T(8,128)}, f32[1024,128]{1,0:T(8,128)}) custom-call(f32[1024,128]{1,0:T(8,128)} %get-tuple-element.4.a_in, f32[1024,128]{1,0:T(8,128)} %get-tuple-element.5.b_in), custom_call_target="tpu_custom_call" | custom-call | tf_op jit(solution)/shard_map/pallas_call | solution.py:475

commit v4 on v3

--- a/solution.py
+++ b/solution.py
@@ -11,6 +11,10 @@
 F32 = jnp.float32
 BF16 = jnp.bfloat16
 ITERS = 2
+PIECES = 2
+PIECE = 64 // PIECES
+PARTS = 4
+PART = 128 // PARTS
 ROWS = 1024
 K = 128
 N = 8192
@@ -39,8 +43,8 @@
     dos, traits, coef, tested, ds, dts, tts, weights, loco_w,
     part, coresum, corebuf, crecv, rfull, gpart, grecv, gfull, score,
     acc, own0, own1, gmask, omask, tcol, tsq_recv, lsq_recv, scal,
-    load_sem, core_send, core_recv, far_send, crs_send, crs_recv, cag_send, cag_recv, fwd_send, fwd_recv,
-    far_recv, srs_send, srs_recv, sag_send, sag_recv, scal_send, scal_recv, small_send, small_recv, out_sem,
+    load_sem, core_send, core_recv, crs_send, crs_recv, cag_send, cag_recv, fwd_send, fwd_recv,
+    srs_send, srs_recv, sag_send, sag_recv, scal_send, scal_recv, small_send, small_recv, out_sem,
 ):
     s = lax.axis_index("samp")
     c = lax.axis_index("chrom")
@@ -51,7 +55,6 @@
     z = q % 2
     me = s * 16 + c
     partner = (s, q * 2 + other)
-    opposite = (x + 2) % 4 * 2 + (1 - z)
 
     def chip(dx, dz):
         return (x + dx) % 4 * 2 + (z + dz) % 2
@@ -59,7 +62,7 @@
     def samp_peer(k):
         return (s // 4 + k // 4) % 2 * 4 + (s + k) % 4
 
-    far_first = [(2, 0), (1, 1), (3, 1), (1, 0), (3, 0), (0, 1)]
+    far_first = [(2, 1), (2, 0), (1, 1), (3, 1), (1, 0), (3, 0), (0, 1)]
     samp_order = (6, 2, 5, 7, 3, 1, 4)
 
     y = s % 4
@@ -81,9 +84,8 @@
     bar = pltpu.get_barrier_semaphore()
     for k in samp_order:
         pl.semaphore_signal(bar, inc=1, device_id=(samp_peer(k), c), device_id_type=MESH)
-    for dx, dz in [(2, 1)] + far_first:
+    for dx, dz in far_first:
         pl.semaphore_signal(bar, inc=1, device_id=(s, chip(dx, dz) * 2 + core), device_id_type=MESH)
-    pl.semaphore_signal(bar, inc=1, device_id=(s, opposite * 2 + other), device_id_type=MESH)
     pl.semaphore_signal(bar, inc=1, device_id=partner, device_id_type=MESH)
 
     order = [other * 2, other * 2 + 1, core * 2, core * 2 + 1]
@@ -120,79 +122,68 @@
         out = jnp.dot(lhs[chunk, :, depth], weights[depth, 0:256], preferred_element_type=F32)
         return (out[:256, :K] + (out[:256, K:] + out[256:, K:])) + out[256:, :K]
 
-    def rows32(t, u, half):
-        return pl.ds(pl.multiple_of(half * 512 + u * 256 + t * 32, 32), 32)
+    def piece(t, u, half):
+        return pl.ds(pl.multiple_of(half * 512 + u * (512 // PIECES) + t * PIECE, PIECE), PIECE)
 
     def chrom_rs(ph, compute, done, filler=None):
-        cut = pl.ds(pl.multiple_of(opposite * 32, 32), 32)
-        mine = pl.ds(pl.multiple_of(q * 32, 32), 32)
         for i, chunk in enumerate(order):
-            u = i % 2
             part[ph, i] = compute(i, chunk)
             if i < 2:
-                remote(part.at[ph, i], corebuf.at[ph, u], core_send.at[ph, u], core_recv.at[ph, u], partner).start()
-                remote(part.at[ph, i, cut], crecv.at[ph, u, 8], far_send.at[ph], crs_recv.at[ph, u],
-                       (s, opposite * 2 + other)).start()
-            else:
-                remote(part.at[ph, i, cut], crecv.at[ph, u, q], far_send.at[ph], crs_recv.at[ph, u],
-                       (s, opposite * 2 + core)).start()
-        for u in range(2):
-            wait_bytes(corebuf.at[ph, u], core_recv.at[ph, u])
-            coresum[ph, u] = part[ph, 2 + u] + corebuf[ph, u]
-            for dx, dz in far_first:
-                t = chip(dx, dz)
-                remote(coresum.at[ph, u, pl.ds(pl.multiple_of(t * 32, 32), 32)], crecv.at[ph, u, q],
-                       crs_send.at[ph], crs_recv.at[ph, u], (s, t * 2 + core)).start()
-            crecv[ph, u, q] = coresum[ph, u, mine, :]
+                remote(part.at[ph, i], corebuf.at[ph, i], core_send.at[ph, i], core_recv.at[ph, i], partner).start()
+        for i in range(2):
+            wait_bytes(corebuf.at[ph, i], core_recv.at[ph, i])
+            coresum[ph, i * 256:i * 256 + 256, :] = part[ph, 2 + i] + corebuf[ph, i]
+            for u in range(i * PIECES // 2, (i + 1) * PIECES // 2):
+                for dx, dz in far_first:
+                    t = chip(dx, dz)
+                    remote(coresum.at[ph, piece(t, u, 0)], crecv.at[ph, u, q],
+                           crs_send.at[ph], crs_recv.at[ph, u], (s, t * 2 + core)).start()
+                crecv[ph, u, q] = coresum[ph, piece(q, u, 0), :]
         if filler is not None:
             filler()
-        for u in range(2):
-            wait_bytes(crecv.at[ph, u, pl.ds(0, 8)], crs_recv.at[ph, u])
+        for u in range(PIECES):
+            wait_bytes(crecv.at[ph, u, pl.ds(0, 7)], crs_recv.at[ph, u])
             total = crecv[ph, u, 0]
-            for k in range(1, 9):
+            for k in range(1, 8):
                 total = total + crecv[ph, u, k]
             done(u, total)
 
     def chrom_ag_send(a, full, u):
-        mine = rows32(q, u, core)
-        remote(full.at[mine], full.at[mine], cag_send.at[a], cag_recv.at[a, u, q],
-               (s, opposite * 2 + core)).start()
-        remote(full.at[mine], full.at[mine], cag_send.at[a], far_recv.at[a, u],
-               (s, opposite * 2 + other)).start()
+        mine = piece(q, u, core)
         for dx, dz in far_first:
             remote(full.at[mine], full.at[mine], cag_send.at[a], cag_recv.at[a, u, q],
                    (s, chip(dx, dz) * 2 + core)).start()
         remote(full.at[mine], full.at[mine], fwd_send.at[a], fwd_recv.at[a, u], partner).start()
 
     def chrom_ag_wait(a, full, use):
-        for u in range(2):
+        for u in range(PIECES):
             for dx, dz in reversed(far_first):
                 t = chip(dx, dz)
-                rows = rows32(t, u, core)
+                rows = piece(t, u, core)
                 wait_bytes(full.at[rows], cag_recv.at[a, u, t])
                 remote(full.at[rows], full.at[rows], fwd_send.at[a], fwd_recv.at[a, u], partner).start()
-            wait_bytes(full.at[rows32(0, u, core)], cag_recv.at[a, u, opposite])
         use(core * 2)
         use(core * 2 + 1)
-        for u in range(2):
-            wait_bytes(full.at[rows32(0, u, core)], far_recv.at[a, u])
-            wait_bytes(full.at[pl.ds(0, 224)], fwd_recv.at[a, u])
-            use(other * 2 + u)
+        for i in range(2):
+            for u in range(i * PIECES // 2, (i + 1) * PIECES // 2):
+                wait_bytes(full.at[pl.ds(0, 8 * PIECE)], fwd_recv.at[a, u])
+            use(other * 2 + i)
 
     def srows(t, u):
-        return pl.ds(pl.multiple_of(u * 256 + t * 32, 32), 32)
+        return pl.ds(pl.multiple_of(u * (1024 // PARTS) + t * PART, PART), PART)
 
     def samp_rs(ph, compute, done, filler=None):
-        for u in range(4):
-            gpart[ph, u] = compute(u)
-            for k in samp_order:
-                t = samp_peer(k)
-                remote(gpart.at[ph, u, pl.ds(pl.multiple_of(t * 32, 32), 32)], grecv.at[ph, u, s],
-                       srs_send.at[ph], srs_recv.at[ph, u], (t, c)).start()
-            grecv[ph, u, s] = gpart[ph, u, pl.ds(pl.multiple_of(s * 32, 32), 32), :]
+        for v in range(4):
+            gpart[ph, v * 256:v * 256 + 256, :] = compute(v)
+            for u in range(v * PARTS // 4, (v + 1) * PARTS // 4):
+                for k in samp_order:
+                    t = samp_peer(k)
+                    remote(gpart.at[ph, srows(t, u)], grecv.at[ph, u, s],
+                           srs_send.at[ph], srs_recv.at[ph, u], (t, c)).start()
+                grecv[ph, u, s] = gpart[ph, srows(s, u), :]
         if filler is not None:
             filler()
-        for u in range(4):
+        for u in range(PARTS):
             wait_bytes(grecv.at[ph, u, pl.ds(0, 7)], srs_recv.at[ph, u])
             total = grecv[ph, u, 0]
             for k in range(1, 8):
@@ -204,7 +195,7 @@
             remote(src, dst, sag_send.at[ph], sag_recv.at[ph, u], (samp_peer(k), c)).start()
 
     def samp_ag_wait(ph, u):
-        wait_bytes(gfull.at[0, pl.ds(0, 224)], sag_recv.at[ph, u])
+        wait_bytes(gfull.at[0, pl.ds(0, 7 * PART)], sag_recv.at[ph, u])
 
     def prepare_transposed():
         @pl.loop(0, 16)
@@ -217,8 +208,6 @@
             dts[j, 256:512, rows] = low
 
     def prepare_tested():
-        load_tested.wait()
-
         @pl.loop(0, 16)
         def _(b):
             i, j = b // 4, b % 4
@@ -227,6 +216,7 @@
             tts[j, :, rows] = tested[rows, cols].astype(F32).T.astype(BF16)
 
     def prepare_tsq():
+        load_tested.wait()
         for b in range(8):
             def add(i, acc):
                 value = tested[pl.ds(pl.multiple_of(i * 128, 128), 128), b * 128:(b + 1) * 128].astype(F32)
@@ -263,7 +253,7 @@
         ds[chunk, 256:512, :] = low
         value = chunk_dot(ds, chunk, weights[:, 0:256])
         if i == 0:
-            pl.semaphore_wait(bar, 16)
+            pl.semaphore_wait(bar, 15)
         return value
 
     def plain_compute(i, chunk):
@@ -275,12 +265,12 @@
         def residual_done(u, total):
             if it == 0 and u == 0:
                 load_traits.wait()
-            rows = rows32(q, u, core)
+            rows = piece(q, u, core)
             rfull[it, rows, :] = traits[rows, :] - total
             chrom_ag_send(it, rfull.at[it], u)
 
         chrom_rs(2 * it, first_compute if it == 0 else plain_compute, residual_done,
-                 prepare_transposed if it == 0 else prepare_tsq)
+                 prepare_transposed if it == 0 else None)
         seen = []
 
         def use_residual(chunk):
@@ -304,30 +294,31 @@
             gfull[it, srows(s, u), :] = grad
             samp_ag_send(it, gfull.at[it, srows(s, u)], gfull.at[it, srows(s, u)], u)
 
-        samp_rs(it, lambda v: acc[v, :, 0:K] + part_dot(dts, v, seen[3]), gradient_done,
-                prepare_masks if it == 0 else prepare_tcol)
-        if it == 0:
-            prepare_tested()
+        samp_rs(it, lambda v: acc[v, :, 0:K] + part_dot(dts, v, seen[3]), gradient_done)
         for u in range(4):
-            samp_ag_wait(it, u)
+            for w in range(u * PARTS // 4, (u + 1) * PARTS // 4):
+                samp_ag_wait(it, w)
             for b in (2 * u, 2 * u + 1):
                 set_weights(b, gfull[it, b * 128:b * 128 + 128, :])
             if u < 3:
                 for v in range(4):
                     value = part_dot(ds, v, slice(u * 256, u * 256 + 256))
                     acc[v, :, 0:K] = value if u == 0 else acc[v, :, 0:K] + value
-        g_row = (squares[0] + squares[1]) + (squares[2] + squares[3])
+        g_row = sum(squares[1:], squares[0])
         g_row = g_row + pltpu.roll(g_row, 64, 1)
         image_squares = []
         chrom_rs(2 * it + 1, lambda i, chunk: acc[chunk, :, 0:K] + part_dot(ds, chunk, slice(768, 1024)),
-                 lambda u, total: image_squares.append(jnp.sum(total * total, axis=0, keepdims=True)))
-        i_row = image_squares[0] + image_squares[1]
+                 lambda u, total: image_squares.append(jnp.sum(total * total, axis=0, keepdims=True)),
+                 prepare_tsq if it == 0 else None)
+        i_row = sum(image_squares[1:], image_squares[0])
         i_row = i_row + pltpu.roll(i_row, 64, 1)
         scal[it, pl.ds(me, 1), :] = jnp.where(lane < 64, g_row, i_row)
 
         for far_s, far_c in everyone:
             remote(scal.at[it, pl.ds(me, 1)], scal.at[it, pl.ds(me, 1)], scal_send.at[it], scal_recv.at[it],
                    (far_s, far_c)).start()
+        for work in ((prepare_tested,), (prepare_masks, prepare_tcol))[it]:
+            work()
         wait_bytes(scal.at[it, pl.ds(0, 127)], scal_recv.at[it])
         sums = jnp.sum(scal[it], axis=0, keepdims=True)
         grad_sq = jnp.sum(jnp.where(lane < 64, sums, 0.0), axis=1, keepdims=True)
@@ -339,28 +330,24 @@
             moved = coef[rows, :] + step * gfull[it, rows, :]
             length = jnp.sqrt(jnp.sum(moved * moved, axis=1, keepdims=True))
             new = moved * (jnp.maximum(length - limit, 0.0) / jnp.maximum(length, limit))
-            if it + 1 < ITERS:
-                coef[rows, :] = new
-                set_weights(b, new)
-            else:
-                second = new * gmask[rows, :]
-                set_weights(b, new * (1.0 - gmask[rows, :]), 0)
-                set_weights(b, second, 256)
-
-    def final_compute(i, chunk):
-        rows = pl.ds(pl.multiple_of(chunk * 256, 256), 256)
-        a = chunk_dot(ds, chunk, weights[:, 0:256])
-        b = chunk_dot(ds, chunk, weights[:, 256:512])
-        own0[rows, :] = a
-        own1[rows, :] = b
-        return a + b
+            coef[rows, :] = new
+            set_weights(b, new)
+
+    def own_parts():
+        for b in range(8):
+            set_weights(b, coef[b * 128:b * 128 + 128, :] * (1.0 - gmask[b * 128:b * 128 + 128, :]), 256)
+        for i, chunk in enumerate(order):
+            rows = rows256(chunk)
+            value = chunk_dot(ds, chunk, weights[:, 256:512])
+            own0[rows, :] = value
+            own1[rows, :] = part[4, i] - value
 
     def last_residual_done(u, total):
-        rows = rows32(q, u, core)
+        rows = piece(q, u, core)
         rfull[2, rows, :] = traits[rows, :] - total
         chrom_ag_send(2, rfull.at[2], u)
 
-    chrom_rs(4, final_compute, last_residual_done)
+    chrom_rs(4, plain_compute, last_residual_done, own_parts)
     sq = []
     seen_last = []
 
@@ -408,8 +395,9 @@
         samp_ag_send(2, score.at[u], scores_out.at[rows], u)
         pltpu.make_async_copy(score.at[u], scores_out.at[rows], out_sem.at[1 + u]).start()
 
-    samp_rs(2, products, score_done, send_squares)
-    for u in range(4):
+    send_squares()
+    samp_rs(2, products, score_done)
+    for u in range(PARTS):
         samp_ag_wait(2, u)
         wait_bytes(score.at[u], out_sem.at[1 + u])
     give_resid.wait()
@@ -417,11 +405,10 @@
     for ph in range(5):
         for u in range(2):
             wait_bytes(corebuf.at[ph, u], core_send.at[ph, u])
-        wait_bytes(rfull.at[0, pl.ds(0, 128)], far_send.at[ph])
-        wait_bytes(rfull.at[0, pl.ds(0, 384)], crs_send.at[ph])
+        wait_bytes(rfull.at[0, pl.ds(0, 448)], crs_send.at[ph])
     for a in range(3):
-        wait_bytes(rfull.at[0, pl.ds(0, 512)], cag_send.at[a])
-        wait_bytes(rfull.at[0, pl.ds(0, 448)], fwd_send.at[a])
+        wait_bytes(rfull.at[0, pl.ds(0, 448)], cag_send.at[a])
+        wait_bytes(rfull.at[0, pl.ds(0, 512)], fwd_send.at[a])
         wait_bytes(rfull.at[0, pl.ds(0, 896)], srs_send.at[a])
         wait_bytes(rfull.at[0, pl.ds(0, 896)], sag_send.at[a])
     for it in range(ITERS):
@@ -459,14 +446,14 @@
             V((1024, 1024), F32), V((1024, K), F32), V((1024, K), F32), V((1024, 1024), BF16),
             V((4, 512, 1024), BF16), V((4, 512, 1024), BF16), V((4, 256, 1024), BF16),
             V((1024, 512), BF16), V((1024, 256), BF16),
-            V((5, 4, 256, K), F32), V((5, 2, 256, K), F32), V((5, 2, 256, K), F32), V((5, 2, 9, 32, K), F32),
-            V((3, 1024, K), F32), V((3, 4, 256, K), F32), V((3, 4, 8, 32, K), F32), V((2, 1024, K), F32),
-            V((4, 32, K), F32), V((4, 256, 2 * K), F32),
+            V((5, 4, 256, K), F32), V((5, 512, K), F32), V((5, 2, 256, K), F32), V((5, PIECES, 8, PIECE, K), F32),
+            V((3, 1024, K), F32), V((3, 1024, K), F32), V((3, PARTS, 8, PART, K), F32), V((2, 1024, K), F32),
+            V((PARTS, PART, K), F32), V((4, 256, 2 * K), F32),
             V((1024, K), F32), V((1024, K), F32), V((1024, K), F32), V((1024, K), F32), V((1024, K), F32),
             V((8, 8, K), F32), V((8, 2, K), F32), V((2, 128, K), F32),
-            DMA((8,)), DMA((5, 2)), DMA((5, 2)), DMA((5,)), DMA((5,)), DMA((5, 2)), DMA((3,)), DMA((3, 2, 8)),
-            DMA((3,)), DMA((3, 2)), DMA((3, 2)), DMA((3,)), DMA((3, 4)), DMA((3,)), DMA((3, 4)),
-            DMA((2,)), DMA((2,)), DMA((2,)), DMA((2,)), DMA((5,)),
+            DMA((8,)), DMA((5, 2)), DMA((5, 2)), DMA((5,)), DMA((5, PIECES)), DMA((3,)), DMA((3, PIECES, 8)),
+            DMA((3,)), DMA((3, PIECES)), DMA((3,)), DMA((3, PARTS)), DMA((3,)), DMA((3, PARTS)),
+            DMA((2,)), DMA((2,)), DMA((2,)), DMA((2,)), DMA((1 + PARTS,)),
         ],
         compiler_params=pltpu.CompilerParams(
             collective_id=0, has_side_effects=True, vmem_limit_bytes=62 * 1024 * 1024

time: 129 us -> 124 us (0.961)
  Pallas kernels: 128 us -> 123 us
    pallas_call x1, Pallas kernels: 126 us -> 121 us  [body(): pl.pallas_call(kernel, out_shape=(out, out), in_specs=[any_spec, any_spec...]
where the time goes in v4:
time: 124 us
  Pallas kernels  123 us (99%)
    pallas_call x1, Pallas kernels, body(): pl.pallas_call(kernel, out_shape=(out, out), in_specs=[any_spec, any_spec...  121 us

profile of v4, /device:TPU:1, one launch (start us, length us, event | category | flops | bytes accessed | tf_op | source)
XLA Modules:
  0.0 123.9 jit_solution(1916662351216675229)
XLA Ops:
  0.6 121.2 %shard_map.77 = (f32[1024,128]{1,0:T(8,128)}, f32[1024,128]{1,0:T(8,128)}) custom-call(f32[1024,1024]{1,0:T(8,128)} %dos_hbm.1, f32[1024,128]{1,0:T(8,128)} %traits_hbm.1, f32[1024,128]{1,0:T(8,128)} %coef_hbm.1, s32[8,128]{1,0:T(8,128)} %bitcast.2, bf16[1024,1024]{1,0:T(8,128)(2,1)} %tested_hbm.1, s32[8,128]{1,0:T(8,128)} %bitcast.3), custom_call_target="tpu_custom_call" | custom-call | tf_op jit(solution)/shard_map/pallas_call | solution.py:440
  121.8 2.0 %shard_map.78 = (f32[1024,128]{1,0:T(8,128)}, f32[1024,128]{1,0:T(8,128)}) custom-call(f32[1024,128]{1,0:T(8,128)} %get-tuple-element.4.a_in, f32[1024,128]{1,0:T(8,128)} %get-tuple-element.5.b_in), custom_call_target="tpu_custom_call" | custom-call | tf_op jit(solution)/shard_map/pallas_call | solution.py:462

commit v5 on v4

--- a/solution.py
+++ b/solution.py
@@ -44,7 +44,7 @@
     part, coresum, corebuf, crecv, rfull, gpart, grecv, gfull, score,
     acc, own0, own1, gmask, omask, tcol, tsq_recv, lsq_recv, scal,
     load_sem, core_send, core_recv, crs_send, crs_recv, cag_send, cag_recv, fwd_send, fwd_recv,
-    srs_send, srs_recv, sag_send, sag_recv, scal_send, scal_recv, small_send, small_recv, out_sem,
+    srs_send, srs_recv, sag_send, sag_recv, scal_send, scal_recv, small_send, small_recv, out_sem, greet_sem,
 ):
     s = lax.axis_index("samp")
     c = lax.axis_index("chrom")
@@ -82,11 +82,19 @@
         everyone.append((s_of[dz][dy], c_of[dz][dx][dc]))
 
     bar = pltpu.get_barrier_semaphore()
-    for k in samp_order:
-        pl.semaphore_signal(bar, inc=1, device_id=(samp_peer(k), c), device_id_type=MESH)
+    near_samp = (4, 1, 3)
     for dx, dz in far_first:
         pl.semaphore_signal(bar, inc=1, device_id=(s, chip(dx, dz) * 2 + core), device_id_type=MESH)
+    for k in near_samp:
+        pl.semaphore_signal(bar, inc=1, device_id=(samp_peer(k), c), device_id_type=MESH)
     pl.semaphore_signal(bar, inc=1, device_id=partner, device_id_type=MESH)
+
+    def greet(turn):
+        for k in near_samp:
+            pl.semaphore_signal(greet_sem.at[turn], inc=1, device_id=(samp_peer(k), c), device_id_type=MESH)
+
+    def greeted(turn):
+        pl.semaphore_wait(greet_sem.at[turn], 3)
 
     order = [other * 2, other * 2 + 1, core * 2, core * 2 + 1]
     load_coef = pltpu.make_async_copy(coef_hbm, coef, load_sem.at[0])
@@ -94,13 +102,11 @@
     load_dos = []
     for i, chunk in enumerate(order):
         rows = pl.ds(pl.multiple_of(chunk * 256, 256), 256)
-        cp = pltpu.make_async_copy(dos_hbm.at[rows], dos.at[rows], load_sem.at[1 + i])
-        cp.start()
-        load_dos.append(cp)
+        load_dos.append(pltpu.make_async_copy(dos_hbm.at[rows], dos.at[rows], load_sem.at[1 + i]))
+    load_dos[0].start()
+    load_dos[1].start()
     load_traits = pltpu.make_async_copy(traits_hbm, traits, load_sem.at[5])
-    load_traits.start()
     load_tested = pltpu.make_async_copy(tested_hbm, tested, load_sem.at[6])
-    load_tested.start()
 
     def set_weights(block, value, at=0):
         rows = slice(block * 128, block * 128 + 128)
@@ -126,11 +132,7 @@
         return pl.ds(pl.multiple_of(half * 512 + u * (512 // PIECES) + t * PIECE, PIECE), PIECE)
 
     def chrom_rs(ph, compute, done, filler=None):
-        for i, chunk in enumerate(order):
-            part[ph, i] = compute(i, chunk)
-            if i < 2:
-                remote(part.at[ph, i], corebuf.at[ph, i], core_send.at[ph, i], core_recv.at[ph, i], partner).start()
-        for i in range(2):
+        def pass_on(i):
             wait_bytes(corebuf.at[ph, i], core_recv.at[ph, i])
             coresum[ph, i * 256:i * 256 + 256, :] = part[ph, 2 + i] + corebuf[ph, i]
             for u in range(i * PIECES // 2, (i + 1) * PIECES // 2):
@@ -139,6 +141,16 @@
                     remote(coresum.at[ph, piece(t, u, 0)], crecv.at[ph, u, q],
                            crs_send.at[ph], crs_recv.at[ph, u], (s, t * 2 + core)).start()
                 crecv[ph, u, q] = coresum[ph, piece(q, u, 0), :]
+
+        for i, chunk in enumerate(order):
+            part[ph, i] = compute(i, chunk)
+            if i < 2:
+                remote(part.at[ph, i], corebuf.at[ph, i], core_send.at[ph, i], core_recv.at[ph, i], partner).start()
+            elif ph == 0:
+                pass_on(i - 2)
+        if ph > 0:
+            pass_on(0)
+            pass_on(1)
         if filler is not None:
             filler()
         for u in range(PIECES):
@@ -198,7 +210,14 @@
         wait_bytes(gfull.at[0, pl.ds(0, 7 * PART)], sag_recv.at[ph, u])
 
     def prepare_transposed():
-        @pl.loop(0, 16)
+        greet(0)
+        transpose_blocks(0, 8)
+        greeted(0)
+        greet(1)
+        transpose_blocks(8, 16)
+
+    def transpose_blocks(first, last):
+        @pl.loop(first, last)
         def _(b):
             i, j = b // 4, b % 4
             rows = pl.ds(pl.multiple_of(i * 256, 256), 256)
@@ -248,12 +267,18 @@
 
     def first_compute(i, chunk):
         load_dos[i].wait()
+        if i < 2:
+            load_dos[i + 2].start()
+        if i == 2:
+            load_traits.start()
+        if i == 3:
+            load_tested.start()
         high, low = split(dos[pl.ds(pl.multiple_of(chunk * 256, 256), 256), :])
         ds[chunk, 0:256, :] = high
         ds[chunk, 256:512, :] = low
         value = chunk_dot(ds, chunk, weights[:, 0:256])
         if i == 0:
-            pl.semaphore_wait(bar, 15)
+            pl.semaphore_wait(bar, 11)
         return value
 
     def plain_compute(i, chunk):
@@ -285,6 +310,8 @@
                     acc[v, :, 0:K] = value if len(seen) == 1 else acc[v, :, 0:K] + value
 
         chrom_ag_wait(it, rfull.at[it], use_residual)
+        if it == 0:
+            greeted(1)
 
         squares = []
 
@@ -453,7 +480,7 @@
             V((8, 8, K), F32), V((8, 2, K), F32), V((2, 128, K), F32),
             DMA((8,)), DMA((5, 2)), DMA((5, 2)), DMA((5,)), DMA((5, PIECES)), DMA((3,)), DMA((3, PIECES, 8)),
             DMA((3,)), DMA((3, PIECES)), DMA((3,)), DMA((3, PARTS)), DMA((3,)), DMA((3, PARTS)),
-            DMA((2,)), DMA((2,)), DMA((2,)), DMA((2,)), DMA((1 + PARTS,)),
+            DMA((2,)), DMA((2,)), DMA((2,)), DMA((2,)), DMA((1 + PARTS,)), pltpu.SemaphoreType.REGULAR((2,)),
         ],
         compiler_params=pltpu.CompilerParams(
             collective_id=0, has_side_effects=True, vmem_limit_bytes=62 * 1024 * 1024

time: 124 us -> 123 us (level)
  no operation moved by 1% of the time
where the time goes in v5:
time: 123 us
  Pallas kernels  122 us (99%)
    pallas_call x1, Pallas kernels, body(): pl.pallas_call(kernel, out_shape=(out, out), in_specs=[any_spec, any_spec...  120 us

profile of v5, /device:TPU:1, one launch (start us, length us, event | category | flops | bytes accessed | tf_op | source)
XLA Modules:
  0.0 123.2 jit_solution(3461281730880680054)
XLA Ops:
  0.6 120.4 %shard_map.77 = (f32[1024,128]{1,0:T(8,128)}, f32[1024,128]{1,0:T(8,128)}) custom-call(f32[1024,1024]{1,0:T(8,128)} %dos_hbm.1, f32[1024,128]{1,0:T(8,128)} %traits_hbm.1, f32[1024,128]{1,0:T(8,128)} %coef_hbm.1, s32[8,128]{1,0:T(8,128)} %bitcast.2, bf16[1024,1024]{1,0:T(8,128)(2,1)} %tested_hbm.1, s32[8,128]{1,0:T(8,128)} %bitcast.3), custom_call_target="tpu_custom_call" | custom-call | tf_op jit(solution)/shard_map/pallas_call | solution.py:467
  121.0 2.0 %shard_map.78 = (f32[1024,128]{1,0:T(8,128)}, f32[1024,128]{1,0:T(8,128)}) custom-call(f32[1024,128]{1,0:T(8,128)} %get-tuple-element.4.a_in, f32[1024,128]{1,0:T(8,128)} %get-tuple-element.5.b_in), custom_call_target="tpu_custom_call" | custom-call | tf_op jit(solution)/shard_map/pallas_call | solution.py:489

commit v6 on v5

--- a/solution.py
+++ b/solution.py
@@ -38,9 +38,9 @@
 
 
 def kernel(
-    dos_hbm, traits_hbm, coef_hbm, groups_ref, tested_hbm, owners_ref,
+    dos_hbm, traits_hbm, coef_hbm, groups_hbm, tested_hbm, owners_hbm,
     scores_out, resid_out,
-    dos, traits, coef, tested, ds, dts, tts, weights, loco_w,
+    groups_ref, owners_ref, dos, traits, coef, tested, ds, dts, tts, weights, loco_w,
     part, coresum, corebuf, crecv, rfull, gpart, grecv, gfull, score,
     acc, own0, own1, gmask, omask, tcol, tsq_recv, lsq_recv, scal,
     load_sem, core_send, core_recv, crs_send, crs_recv, cag_send, cag_recv, fwd_send, fwd_recv,
@@ -107,6 +107,8 @@
     load_dos[1].start()
     load_traits = pltpu.make_async_copy(traits_hbm, traits, load_sem.at[5])
     load_tested = pltpu.make_async_copy(tested_hbm, tested, load_sem.at[6])
+    load_groups = pltpu.make_async_copy(groups_hbm, groups_ref, load_sem.at[7])
+    load_owners = pltpu.make_async_copy(owners_hbm, owners_ref, load_sem.at[8])
 
     def set_weights(block, value, at=0):
         rows = slice(block * 128, block * 128 + 128)
@@ -246,6 +248,8 @@
             remote(tsq_recv.at[s], tsq_recv.at[s], small_send.at[0], small_recv.at[0], (samp_peer(k), c)).start()
 
     def prepare_masks():
+        load_groups.wait()
+        load_owners.wait()
         for b in range(8):
             rows = slice(b * 128, b * 128 + 128)
             g = (groups_ref[b:b + 1, :] - c * 2).astype(F32)
@@ -273,6 +277,8 @@
             load_traits.start()
         if i == 3:
             load_tested.start()
+            load_groups.start()
+            load_owners.start()
         high, low = split(dos[pl.ds(pl.multiple_of(chunk * 256, 256), 256), :])
         ds[chunk, 0:256, :] = high
         ds[chunk, 256:512, :] = low
@@ -460,16 +466,16 @@
 
 def body(dosages, traits, start_coef, groups, tested, owners):
     any_spec = pl.BlockSpec(memory_space=pl.ANY)
-    vmem_spec = pl.BlockSpec(memory_space=pltpu.VMEM)
     V = pltpu.VMEM
     DMA = pltpu.SemaphoreType.DMA
     out = jax.ShapeDtypeStruct((ROWS, K), F32)
     scores, resid = pl.pallas_call(
         kernel,
         out_shape=(out, out),
-        in_specs=[any_spec, any_spec, any_spec, vmem_spec, any_spec, vmem_spec],
+        in_specs=[any_spec] * 6,
         out_specs=(any_spec, any_spec),
         scratch_shapes=[
+            V((8, K), jnp.int32), V((8, K), jnp.int32),
             V((1024, 1024), F32), V((1024, K), F32), V((1024, K), F32), V((1024, 1024), BF16),
             V((4, 512, 1024), BF16), V((4, 512, 1024), BF16), V((4, 256, 1024), BF16),
             V((1024, 512), BF16), V((1024, 256), BF16),
@@ -478,7 +484,7 @@
             V((PARTS, PART, K), F32), V((4, 256, 2 * K), F32),
             V((1024, K), F32), V((1024, K), F32), V((1024, K), F32), V((1024, K), F32), V((1024, K), F32),
             V((8, 8, K), F32), V((8, 2, K), F32), V((2, 128, K), F32),
-            DMA((8,)), DMA((5, 2)), DMA((5, 2)), DMA((5,)), DMA((5, PIECES)), DMA((3,)), DMA((3, PIECES, 8)),
+            DMA((9,)), DMA((5, 2)), DMA((5, 2)), DMA((5,)), DMA((5, PIECES)), DMA((3,)), DMA((3, PIECES, 8)),
             DMA((3,)), DMA((3, PIECES)), DMA((3,)), DMA((3, PARTS)), DMA((3,)), DMA((3, PARTS)),
             DMA((2,)), DMA((2,)), DMA((2,)), DMA((2,)), DMA((1 + PARTS,)), pltpu.SemaphoreType.REGULAR((2,)),
         ],

time: 123 us -> 123 us (level)
  no operation moved by 1% of the time
where the time goes in v6:
time: 123 us
  Pallas kernels  122 us (99%)
    pallas_call x1, Pallas kernels, body(): pl.pallas_call(kernel, out_shape=(out, out), in_specs=[any_spec] * 6, out...  120 us

profile of v6, /device:TPU:1, one launch (start us, length us, event | category | flops | bytes accessed | tf_op | source)
XLA Modules:
  0.0 122.7 jit_solution(15006605361132937106)
XLA Ops:
  0.6 119.9 %shard_map.77 = (f32[1024,128]{1,0:T(8,128)}, f32[1024,128]{1,0:T(8,128)}) custom-call(f32[1024,1024]{1,0:T(8,128)} %dos_hbm.1, f32[1024,128]{1,0:T(8,128)} %traits_hbm.1, f32[1024,128]{1,0:T(8,128)} %coef_hbm.1, s32[8,128]{1,0:T(8,128)} %bitcast.2, bf16[1024,1024]{1,0:T(8,128)(2,1)} %tested_hbm.1, s32[8,128]{1,0:T(8,128)} %bitcast.3), custom_call_target="tpu_custom_call" | custom-call | tf_op jit(solution)/shard_map/pallas_call | solution.py:472
  120.6 2.0 %shard_map.78 = (f32[1024,128]{1,0:T(8,128)}, f32[1024,128]{1,0:T(8,128)}) custom-call(f32[1024,128]{1,0:T(8,128)} %get-tuple-element.4.a_in, f32[1024,128]{1,0:T(8,128)} %get-tuple-element.5.b_in), custom_call_target="tpu_custom_call" | custom-call | tf_op jit(solution)/shard_map/pallas_call | solution.py:495

commit v7 on v6

--- a/solution.py
+++ b/solution.py
@@ -62,8 +62,8 @@
     def samp_peer(k):
         return (s // 4 + k // 4) % 2 * 4 + (s + k) % 4
 
-    far_first = [(2, 1), (2, 0), (1, 1), (3, 1), (1, 0), (3, 0), (0, 1)]
-    samp_order = (6, 2, 5, 7, 3, 1, 4)
+    far_first = [(2, 1), (1, 1), (3, 1), (2, 0), (0, 1), (1, 0), (3, 0)]
+    samp_order = (6, 5, 7, 2, 4, 1, 3)
 
     y = s % 4
     depth = s // 4 * 2 + z

time: 123 us -> 122 us (level)
    pallas_call x1, Pallas kernels: 120 us -> 119 us  [body(): pl.pallas_call(kernel, out_shape=(out, out), in_specs=[any_spec] * 6, out...]
where the time goes in v7:
time: 122 us; the launch traced here: 121 us
  Pallas kernels  121 us (99%)
    pallas_call x1, Pallas kernels, body(): pl.pallas_call(kernel, out_shape=(out, out), in_specs=[any_spec] * 6, out...  119 us

profile of v7, /device:TPU:1, one launch (start us, length us, event | category | flops | bytes accessed | tf_op | source)
XLA Modules:
  0.0 121.4 jit_solution(1940399391135379246)
XLA Ops:
  0.6 118.6 %shard_map.77 = (f32[1024,128]{1,0:T(8,128)}, f32[1024,128]{1,0:T(8,128)}) custom-call(f32[1024,1024]{1,0:T(8,128)} %dos_hbm.1, f32[1024,128]{1,0:T(8,128)} %traits_hbm.1, f32[1024,128]{1,0:T(8,128)} %coef_hbm.1, s32[8,128]{1,0:T(8,128)} %bitcast.2, bf16[1024,1024]{1,0:T(8,128)(2,1)} %tested_hbm.1, s32[8,128]{1,0:T(8,128)} %bitcast.3), custom_call_target="tpu_custom_call" | custom-call | tf_op jit(solution)/shard_map/pallas_call | solution.py:472
  119.2 2.0 %shard_map.78 = (f32[1024,128]{1,0:T(8,128)}, f32[1024,128]{1,0:T(8,128)}) custom-call(f32[1024,128]{1,0:T(8,128)} %get-tuple-element.4.a_in, f32[1024,128]{1,0:T(8,128)} %get-tuple-element.5.b_in), custom_call_target="tpu_custom_call" | custom-call | tf_op jit(solution)/shard_map/pallas_call | solution.py:495

commit v8 on v7

--- a/solution.py
+++ b/solution.py
@@ -62,8 +62,8 @@
     def samp_peer(k):
         return (s // 4 + k // 4) % 2 * 4 + (s + k) % 4
 
-    far_first = [(2, 1), (1, 1), (3, 1), (2, 0), (0, 1), (1, 0), (3, 0)]
-    samp_order = (6, 5, 7, 2, 4, 1, 3)
+    far_first = [(2, 1), (1, 1), (3, 1), (0, 1), (2, 0), (1, 0), (3, 0)]
+    samp_order = (6, 5, 7, 4, 2, 1, 3)
 
     y = s % 4
     depth = s // 4 * 2 + z

time: 122 us -> 122 us (level)
  no operation moved by 1% of the time
where the time goes in v8:
time: 122 us; the launch traced here: 121 us
  Pallas kernels  121 us (99%)
    pallas_call x1, Pallas kernels, body(): pl.pallas_call(kernel, out_shape=(out, out), in_specs=[any_spec] * 6, out...  119 us

profile of v8, /device:TPU:1, one launch (start us, length us, event | category | flops | bytes accessed | tf_op | source)
XLA Modules:
  0.0 121.4 jit_solution(11653050405620800501)
XLA Ops:
  0.6 118.6 %shard_map.77 = (f32[1024,128]{1,0:T(8,128)}, f32[1024,128]{1,0:T(8,128)}) custom-call(f32[1024,1024]{1,0:T(8,128)} %dos_hbm.1, f32[1024,128]{1,0:T(8,128)} %traits_hbm.1, f32[1024,128]{1,0:T(8,128)} %coef_hbm.1, s32[8,128]{1,0:T(8,128)} %bitcast.2, bf16[1024,1024]{1,0:T(8,128)(2,1)} %tested_hbm.1, s32[8,128]{1,0:T(8,128)} %bitcast.3), custom_call_target="tpu_custom_call" | custom-call | tf_op jit(solution)/shard_map/pallas_call | solution.py:472
  119.2 2.0 %shard_map.78 = (f32[1024,128]{1,0:T(8,128)}, f32[1024,128]{1,0:T(8,128)}) custom-call(f32[1024,128]{1,0:T(8,128)} %get-tuple-element.4.a_in, f32[1024,128]{1,0:T(8,128)} %get-tuple-element.5.b_in), custom_call_target="tpu_custom_call" | custom-call | tf_op jit(solution)/shard_map/pallas_call | solution.py:495
